TPU v7x, 32 devices: a whole 2x2x4 slice. The times are simulated.
32 devices in a mesh: dp: 8 (over z, x), fsdp: 4 (over y, core).
Axes of the slice: x: 2, y: 2, z: 4, core: 2. Of those that a mesh axis runs over, the one named last changes fastest.
Arguments:
- inputs: bfloat16 [32, 1024, 512], P(('dp', 'fsdp')), may hold values from -6 to 6
- noisy_ids: int32 [32, 1024], P(('dp', 'fsdp')), may hold values from 0 to 26
- timesteps: int32 [32, 4], P(('dp', 'fsdp')), may hold values from 0 to 999
- doc_lens: int32 [32, 4], P(('dp', 'fsdp')), may hold values from 0 to 1024, as said below
- cotangent: bfloat16 [32, 1024, 512], P(('dp', 'fsdp')), may hold values from -6 to 6
- params: float32 [3296768], P(('dp', 'fsdp'))
- momentum: float32 [3296768], P(('dp', 'fsdp'))
- average: float32 [3296768], P(('dp', 'fsdp'))
Outputs:
- activations: bfloat16 [32, 1024, 512], P(('dp', 'fsdp'))
- input_grad: float32 [32, 1024, 512], P(('dp', 'fsdp'))
- new_params: float32 [3296768], P(('dp', 'fsdp'))
- new_momentum: float32 [3296768], P(('dp', 'fsdp'))
- new_average: float32 [3296768], P(('dp', 'fsdp'))
- params_low: bfloat16 [3296768], P(('dp', 'fsdp'))
Inputs may be any that keep to these rules, and one draw needn't show every extreme that they name: Each row is either long, with doc_lens[r] = [L, 0, 0, 0] and L from 512 to 1024, or short, with every entry from 128 to 256. In every draw some row is long with L = 1024 and some short row has a slot of exactly 256.
All inputs are finite; a program needn't handle non-finite values.
Results may differ from a plain program's by a relative error of at most 0.011.
Values may be sent and summed in bfloat16 or wider, within the bound.
A program may use at most 192 MiB of HBM per device.

v0:
```python
import math

import jax
import jax.numpy as jnp
from jax import lax
from jax.experimental import pallas as pl
from jax.experimental.pallas import tpu as pltpu
from jax.sharding import PartitionSpec as P

MOMENTUM_RATE = 0.9
LEARN_RATE = 0.02
AVERAGE_RATE = 0.8
EPSILON = 1e-5
MESH = pl.DeviceIdType.MESH
ROW = 512
TILE = 16
BF = jnp.bfloat16
F32 = jnp.float32


class Plan:
    def __init__(self, ndp, nfs, total):
        self.nx, self.ny, self.nc = 2, nfs // 2, 2
        self.nz = ndp // 2
        self.count = ndp * nfs
        self.share = total // self.count
        self.total = total
        self.starts = [self.start(i) for i in range(self.count)]
        ends = [-(-((i + 1) * self.share) // ROW) for i in range(self.count)]
        need = max(e - s for e, s in zip(ends, self.starts))
        self.rows = -(-need // 32) * 32
        self.half = self.rows // 2
        self.padded = max(self.starts) + self.rows

    def start(self, i):
        return ((i * self.share) // (ROW * TILE)) * TILE

    def index(self, z, x, y, c):
        return ((z * self.nx + x) * self.ny + y) * self.nc + c


class Place:
    def __init__(self, plan):
        d = lax.axis_index("dp")
        f = lax.axis_index("fsdp")
        self.plan = plan
        self.z, self.x = d // plan.nx, d % plan.nx
        self.y, self.c = f // plan.nc, f % plan.nc

    def dev(self, z=None, x=None, y=None, c=None):
        z = self.z if z is None else z
        x = self.x if x is None else x
        y = self.y if y is None else y
        c = self.c if c is None else c
        return (z * self.plan.nx + x, y * self.plan.nc + c)

    @property
    def X(self):
        return self.dev(x=1 - self.x)

    @property
    def Y(self):
        return self.dev(y=1 - self.y)

    @property
    def C(self):
        return self.dev(c=1 - self.c)


def greet(place, nz):
    bar = pltpu.get_barrier_semaphore()
    for dev in (place.X, place.Y, place.C):
        pl.semaphore_signal(bar, inc=1, device_id=dev, device_id_type=MESH)
    for s in range(1, nz):
        pl.semaphore_signal(bar, inc=1, device_id=place.dev(z=(place.z + s) % nz), device_id_type=MESH)
    pl.semaphore_wait(bar, 3 + nz - 1)


def rcopy(src, dst, ss, rs, dev):
    return pltpu.make_async_remote_copy(src_ref=src, dst_ref=dst, send_sem=ss, recv_sem=rs, device_id=dev, device_id_type=MESH)


AG_KINDS = 13


def gather_events(plan, layers, g, zs, zr, ps, pr):
    p = Place(plan)
    z, x, y, c, nz, h, n = p.z, p.x, p.y, p.c, plan.nz, plan.half, plan.rows
    A, B, W = pl.ds(0, h), pl.ds(h, h), pl.ds(0, n)

    def at(r, xx, yy, part):
        return g.at[r, xx, yy, c, part]

    def zcopy(r, j, up):
        ref = g.at[r, x, y, c, (A, B)[j]]
        return rcopy(ref, ref, zs.at[r, j, 0 if up else 1], zr.at[r, j], p.dev(z=z + 1 if up else z - 1))

    def cp(r, k):
        table = {
            0: (at(r, x, y, A), p.X), 1: (at(r, x, y, B), p.Y),
            2: (at(r, x, y, A), p.Y), 3: (at(r, x, y, B), p.X),
            4: (at(r, 1 - x, y, A), p.Y), 5: (at(r, x, 1 - y, B), p.X),
            6: (at(r, x, y, W), p.C), 7: (at(r, 1 - x, y, A), p.C), 8: (at(r, x, 1 - y, B), p.C),
            9: (at(r, x, 1 - y, A), p.C), 10: (at(r, 1 - x, 1 - y, A), p.C),
            11: (at(r, 1 - x, y, B), p.C), 12: (at(r, 1 - x, 1 - y, B), p.C),
        }
        ref, dev = table[k]
        return rcopy(ref, ref, ps.at[r, k], pr.at[r, k], dev)

    def stage0(r):
        for j in (0, 1):
            if r < nz - 1:
                @pl.when(z == r)
                def _(): zcopy(r, j, True).start()
            if r > 0:
                @pl.when(z == r)
                def _(): zcopy(r, j, False).start()

    def stage1(r):
        for j in (0, 1):
            @pl.when(z != r)
            def _(): zcopy(r, j, True).wait_recv()
            if r < nz - 1:
                @pl.when((z > r) & (z < nz - 1))
                def _(): zcopy(r, j, True).start()
            if r > 0:
                @pl.when((z < r) & (z > 0))
                def _(): zcopy(r, j, False).start()
            cp(r, j).start()
        for k in (2, 3, 6):
            cp(r, k).start()

    def stage2(r):
        cp(r, 0).wait_recv()
        cp(r, 4).start()
        cp(r, 7).start()
        cp(r, 1).wait_recv()
        cp(r, 5).start()
        cp(r, 8).start()

    def stage3(r):
        for k, kk in ((2, 9), (4, 10), (3, 11), (5, 12)):
            cp(r, k).wait_recv()
            cp(r, kk).start()

    def stage4(r):
        for k in range(6, 13):
            cp(r, k).wait_recv()

    def drain():
        for r in layers:
            for j in (0, 1):
                if r < nz - 1:
                    @pl.when((z >= r) & (z < nz - 1))
                    def _(): zcopy(r, j, True).wait_send()
                if r > 0:
                    @pl.when((z <= r) & (z > 0))
                    def _(): zcopy(r, j, False).wait_send()
            for k in range(AG_KINDS):
                cp(r, k).wait_send()

    return [stage0, stage1, stage2, stage3, stage4], drain


def pipelined(stages, layers):
    order = []
    for t in range(len(layers) + len(stages) - 1):
        for s in reversed(range(len(stages))):
            j = t - s
            if 0 <= j < len(layers):
                order.append((stages[s], layers[j]))
    return order


def gather_scratch(plan):
    nz = plan.nz
    D = pltpu.SemaphoreType.DMA
    return [D((nz, 2, 2)), D((nz, 2)), D((nz, AG_KINDS)), D((nz, AG_KINDS))]


def assemble(plan, g, out, write=None):
    n = plan.rows
    for i in range(plan.count):
        cc = i % 2; yy = (i // 2) % 2; xx = (i // 4) % 2; zz = i // 8
        s = plan.starts[i]
        e = plan.starts[i + 1] if i + 1 < plan.count else plan.padded
        head = g[zz, xx, yy, cc, 0:TILE, :]
        if i:
            j = i - 1
            d = s - plan.starts[j]
            if d < n:
                head = head + g[j // 8, (j // 4) % 2, (j // 2) % 2, j % 2, d:d + TILE, :]
        out[s:s + TILE, :] = head
        if e - s > TILE:
            out[s + TILE:e, :] = g[zz, xx, yy, cc, TILE:e - s, :]


def gather_all(plan, chunk, cid):
    nz, n = plan.nz, plan.rows
    layers = list(range(nz))

    def kern(chunk_ref, out_ref, g, zs, zr, ps, pr, ls):
        p = Place(plan)
        greet(p, nz)
        cpy = pltpu.make_async_copy(chunk_ref, g.at[p.z, p.x, p.y, p.c], ls)
        cpy.start(); cpy.wait()
        stages, drain = gather_events(plan, layers, g, zs, zr, ps, pr)
        for st, r in pipelined(stages, layers):
            st(r)
        assemble(plan, g, out_ref)
        drain()

    return pl.pallas_call(
        kern, out_shape=jax.ShapeDtypeStruct((plan.padded, ROW), BF),
        in_specs=[pl.BlockSpec(memory_space=pltpu.VMEM)],
        out_specs=pl.BlockSpec(memory_space=pltpu.VMEM),
        scratch_shapes=[pltpu.VMEM((nz, 2, 2, 2, n, ROW), BF)] + gather_scratch(plan) + [pltpu.SemaphoreType.DMA],
        compiler_params=pltpu.CompilerParams(collective_id=cid, has_side_effects=True, vmem_limit_bytes=60 << 20),
        name="gather_all",
    )(chunk)


def reduce_events(plan, layers, src, cb, pa, pb, p2, zb, cs, cr, ps, pr, zs, zr):
    p = Place(plan)
    z, x, y, c, nz, h, n = p.z, p.x, p.y, p.c, plan.nz, plan.half, plan.rows

    def rows(r, xx, yy, cc):
        i = plan.index(r, xx, yy, cc)
        return pl.ds(pl.multiple_of(((i * plan.share) // (ROW * TILE)) * TILE, TILE), n)

    def ccopy(r, xx, yy):
        return rcopy(src.at[rows(r, xx, yy, 1 - c)], cb.at[r, xx, yy], cs.at[r, xx, yy], cr.at[r, xx, yy], p.C)

    def cp(r, k):
        table = {
            0: (cb.at[r, :, 1 - y, pl.ds(0, h)], pa.at[r], p.Y),
            1: (cb.at[r, 1 - x, :, pl.ds(h, h)], pb.at[r], p.X),
            2: (pa.at[r, 1 - x], p2.at[r, pl.ds(0, h)], p.X),
            3: (pb.at[r, 1 - y], p2.at[r, pl.ds(h, h)], p.Y),
        }
        s, d, dev = table[k]
        return rcopy(s, d, ps.at[r, k], pr.at[r, k], dev)

    def zcopy(r):
        return rcopy(p2.at[r], zb.at[z], zs.at[r], zr.at[z], p.dev(z=r))

    def zwait(s):
        return rcopy(p2.at[0], zb.at[s], zs.at[0], zr.at[s], p.dev(z=s))

    def stage0(r):
        for xx in (0, 1):
            for yy in (0, 1):
                ccopy(r, xx, yy).start()

    def stage1(r):
        for xx in (0, 1):
            for yy in (0, 1):
                ccopy(r, xx, yy).wait_recv()
                cb[r, xx, yy] = (cb[r, xx, yy].astype(F32) + src[rows(r, xx, yy, c), :].astype(F32)).astype(BF)
        cp(r, 0).start()
        cp(r, 1).start()

    def stage2(r):
        cp(r, 0).wait_recv()
        for xx in (0, 1):
            pa[r, xx] = (pa[r, xx].astype(F32) + cb[r, xx, y, 0:h].astype(F32)).astype(BF)
        cp(r, 2).start()
        cp(r, 1).wait_recv()
        for yy in (0, 1):
            pb[r, yy] = (pb[r, yy].astype(F32) + cb[r, x, yy, h:n].astype(F32)).astype(BF)
        cp(r, 3).start()

    def stage3(r):
        cp(r, 2).wait_recv()
        p2[r, 0:h] = (p2[r, 0:h].astype(F32) + pa[r, x].astype(F32)).astype(BF)
        cp(r, 3).wait_recv()
        p2[r, h:n] = (p2[r, h:n].astype(F32) + pb[r, y].astype(F32)).astype(BF)
        @pl.when(z != r)
        def _(): zcopy(r).start()

    def finish(out, mine):
        out[...] = p2[mine].astype(F32)
        for s in range(nz):
            @pl.when(z != s)
            def _():
                zwait(s).wait_recv()
                out[...] += zb[s].astype(F32)

    def drain():
        for r in layers:
            for xx in (0, 1):
                for yy in (0, 1):
                    ccopy(r, xx, yy).wait_send()
            for k in range(4):
                cp(r, k).wait_send()
            @pl.when(z != r)
            def _(): zcopy(r).wait_send()

    return [stage0, stage1, stage2, stage3], finish, drain


def reduce_scratch(plan):
    nz, n, h = plan.nz, plan.rows, plan.half
    D = pltpu.SemaphoreType.DMA
    return [pltpu.VMEM((nz, 2, 2, n, ROW), BF), pltpu.VMEM((nz, 2, h, ROW), BF), pltpu.VMEM((nz, 2, h, ROW), BF),
            pltpu.VMEM((nz, n, ROW), BF), pltpu.VMEM((nz, n, ROW), BF),
            D((nz, 2, 2)), D((nz, 2, 2)), D((nz, 4)), D((nz, 4)), D((nz,)), D((nz,))]


def reduce_all(plan, src, cid):
    nz, n = plan.nz, plan.rows
    layers = list(range(1, nz)) + [0]

    def kern(src_ref, out_ref, *rest):
        p = Place(plan)
        greet(p, nz)
        stages, finish, drain = reduce_events(plan, layers, src_ref, *rest)
        for st, r in pipelined(stages, layers):
            st(r)
        finish(out_ref, p.z)
        drain()

    return pl.pallas_call(
        kern, out_shape=jax.ShapeDtypeStruct((n, ROW), F32),
        in_specs=[pl.BlockSpec(memory_space=pltpu.VMEM)],
        out_specs=pl.BlockSpec(memory_space=pltpu.VMEM),
        scratch_shapes=reduce_scratch(plan),
        compiler_params=pltpu.CompilerParams(collective_id=cid, has_side_effects=True, vmem_limit_bytes=60 << 20),
        name="reduce_all",
    )(src)

T = 1024
D = 512
BLK = 256
NB = T // BLK
PAIRS = 4
ROW_O, ROW_UP, ROW_DOWN, ROW_T, ROW_C, ROW_V = 1536, 2048, 4096, 6144, 6400, 6427
TAIL = 48
SCALE = 0.125
VMEM_LIMIT = 63 << 20


def mm(a, b):
    return lax.dot_general(a, b, (((1,), (0,)), ((), ())), preferred_element_type=F32)


def mm_nt(a, b):
    return lax.dot_general(a, b, (((1,), (1,)), ((), ())), preferred_element_type=F32)


def mm_tn(a, b):
    return lax.dot_general(a, b, (((0,), (0,)), ((), ())), preferred_element_type=F32)


def norm(h):
    mean = jnp.mean(h, axis=-1, keepdims=True)
    cen = h - mean
    inv = lax.rsqrt(jnp.mean(cen * cen, axis=-1, keepdims=True) + EPSILON)
    return cen * inv, inv


def norm_back(dn, n, inv):
    return (dn - jnp.mean(dn, axis=-1, keepdims=True) - n * jnp.mean(dn * n, axis=-1, keepdims=True)) * inv


def valid_len(lens, b):
    long = lens[0, 1] == 0
    return jnp.where(long, lens[0, 0] - b * BLK, lens[0, b])


def lane_half(par):
    lane = lax.broadcasted_iota(jnp.int32, (1, 128), 1)
    return (lane >= 64) if par else (lane < 64)


def key_bias(lens, qb):
    long = lens[0, 1] == 0
    cols = []
    it = lax.broadcasted_iota(jnp.int32, (BLK, 1), 0)
    for kb in range(NB):
        thr = jnp.where(long | (qb == kb), valid_len(lens, kb), 0)
        cols.append(jnp.where(it < thr, 0.0, -1e30).astype(F32))
    return jnp.concatenate(cols, axis=0)


def unpack(w, base, n, wf, to):
    for j in range(4):
        wf[j, 0:512 * n, :] = w[base:base + 512 * n, 128 * j:128 * j + 128].astype(F32)
    for c in range(n):
        for j in range(4):
            to[c, :, 128 * j:128 * j + 128] = wf[j, pl.ds(c, 512, stride=n), :].astype(BF)


def put(wf, c, n, val):
    for j in range(4):
        wf[j, pl.ds(c, 512, stride=n), :] = val[:, 128 * j:128 * j + 128]


def take(wf, n, out, base):
    for j in range(4):
        out[base:base + 512 * n, 128 * j:128 * j + 128] = wf[j, 0:512 * n, :].astype(BF)


def fwd_body(lens, x, ids, feat, w, resid0, attn_in, qkv, attended, lse, wf, wq, ft):
    unpack(w, 0, 3, wf, wq)
    ctab = w[ROW_C:ROW_C + 32, :]
    vecs = w[ROW_C + 16:ROW_C + TAIL, :].astype(F32)
    o = ROW_V - ROW_C - 16
    g1, b1, bq, bv = vecs[o:o + 1], vecs[o + 1:o + 2], vecs[o + 4:o + 5], vecs[o + 5:o + 6]
    ft[...] = mm(feat[...], w[ROW_T:ROW_T + 256, :])
    long = lens[0, 1] == 0

    def block(b, _):
        r0 = pl.multiple_of(b * BLK, BLK)
        rows = pl.ds(r0, BLK)
        oh = (lax.broadcasted_iota(jnp.int32, (32, BLK), 0) == ids[0:1, rows]).astype(F32).astype(BF)
        side = mm_tn(oh, ctab)
        slot = jnp.where(long, 0, b)
        h = x[rows, :].astype(F32) + (side + ft[pl.ds(slot, 1), :])
        resid0[rows, :] = h
        n, _i = norm(h)
        a = (n * g1 + b1).astype(BF)
        attn_in[rows, :] = a
        for c in range(3):
            pr = mm(a, wq[c])
            if c == 0:
                pr = pr + bq
            if c == 2:
                pr = pr + bv
            pr = pr.astype(BF)
            for j in range(4):
                qkv[4 * c + j, rows, :] = pr[:, 128 * j:128 * j + 128]
        return 0

    lax.fori_loop(0, NB, block, 0)

    ones = jnp.ones((T, 128), BF)

    def attend(i, _):
        pair, qb = lax.div(i, NB), lax.rem(i, NB)
        rows = pl.ds(pl.multiple_of(qb * BLK, BLK), BLK)
        q = qkv[pair, rows, :] * jnp.asarray(SCALE, BF)
        k = qkv[PAIRS + pair]
        va = jnp.concatenate([qkv[2 * PAIRS + pair], ones], axis=1)
        bias = key_bias(lens, qb)
        outs = []
        for par in (0, 1):
            qm = jnp.where(lane_half(par), q, jnp.zeros_like(q))
            s = mm_nt(k, qm) + bias
            m = jnp.max(s, axis=0, keepdims=True)
            e = jnp.exp(s - m)
            l = jnp.sum(e, axis=0, keepdims=True)
            lse[pl.ds(2 * pair + par, 1), rows] = m + jnp.log(l)
            oa = mm_tn(e.astype(BF), va)
            outs.append(oa[:, :128] / oa[:, 128:])
        attended[pair, rows, :] = jnp.where(lane_half(0), outs[0], outs[1]).astype(BF)
        return 0

    lax.fori_loop(0, PAIRS * NB, attend, 0)


def vm():
    return pl.BlockSpec(memory_space=pltpu.VMEM)


def sm():
    return pl.BlockSpec(memory_space=pltpu.SMEM)


def forward(lens, x, ids, feat, w):
    S = jax.ShapeDtypeStruct
    return pl.pallas_call(
        fwd_body,
        out_shape=[S((T, D), F32), S((T, D), BF), S((12, T, 128), BF), S((PAIRS, T, 128), BF), S((8, T), F32)],
        in_specs=[sm()] + [vm()] * 4, out_specs=[vm()] * 5,
        scratch_shapes=[pltpu.VMEM((4, 1536, 128), F32), pltpu.VMEM((3, D, D), BF), pltpu.VMEM((8, D), F32)],
        compiler_params=pltpu.CompilerParams(vmem_limit_bytes=VMEM_LIMIT),
        name="forward",
    )(lens, x, ids, feat, w)


def phi_parts(v):
    cdf = 0.5 * (1.0 + lax.erf(v * (2.0 ** -0.5)))
    pdf = jnp.exp(v * v * -0.5) * (1.0 / math.sqrt(2.0 * math.pi))
    return cdf, pdf


def mid_body(lens, resid0, attended, cot, w, out, dres, datt, grads, small, wf, wu, act, dpre, fin, dbr, dff):
    unpack(w, ROW_UP, 4, wf, wu)
    vecs = w[ROW_C + 16:ROW_C + TAIL, :].astype(F32)
    o = ROW_V - ROW_C - 16
    g2, b2, bo, bd = vecs[o + 2:o + 3], vecs[o + 3:o + 4], vecs[o + 6:o + 7], vecs[o + 7:o + 8]
    small[...] = jnp.zeros_like(small)

    def block(b, _):
        rows = pl.ds(pl.multiple_of(b * BLK, BLK), BLK)
        att = jnp.concatenate([attended[j, rows, :] for j in range(PAIRS)], axis=1)
        h = resid0[rows, :] + (mm(att, w[ROW_O:ROW_O + 512, :]) + bo)
        n, inv = norm(h)
        f = (n * g2 + b2).astype(BF)
        fin[rows, :] = f
        ok = lax.broadcasted_iota(jnp.int32, (BLK, 1), 0) < valid_len(lens, b)
        do = jnp.where(ok, cot[rows, :].astype(F32), 0.0)
        d = do.astype(BF)
        dff[rows, :] = d
        small[0:1, :] += jnp.sum(do, axis=0, keepdims=True)
        acc = h + bd
        e2 = jnp.zeros((BLK, D), F32)
        for c in range(4):
            pre = mm(f, wu[c]) + vecs[o + 8 + c:o + 9 + c]
            cdf, pdf = phi_parts(pre)
            a = (pre * cdf).astype(BF)
            wd = w[ROW_DOWN + 512 * c:ROW_DOWN + 512 * c + 512, :]
            dp = (mm_nt(d, wd) * (cdf + pre * pdf)).astype(BF)
            act[c, rows, :] = a
            dpre[c, rows, :] = dp
            small[4 + c:5 + c, :] += jnp.sum(dp.astype(F32), axis=0, keepdims=True)
            acc = acc + mm(a, wd)
            e2 = e2 + mm_nt(dp, wu[c])
        out[rows, :] = acc.astype(BF)
        small[1:2, :] += jnp.sum(e2 * n, axis=0, keepdims=True)
        small[2:3, :] += jnp.sum(e2, axis=0, keepdims=True)
        dr = do + norm_back(e2 * g2, n, inv)
        dres[rows, :] = dr
        db = dr.astype(BF)
        dbr[rows, :] = db
        small[3:4, :] += jnp.sum(db.astype(F32), axis=0, keepdims=True)
        da = mm_nt(db, w[ROW_O:ROW_O + 512, :]).astype(BF)
        for j in range(PAIRS):
            datt[j, rows, :] = da[:, 128 * j:128 * j + 128]
        return 0

    lax.fori_loop(0, NB, block, 0)

    def wgrad(c, _):
        base = pl.multiple_of(ROW_DOWN - ROW_O + 512 * c, 512)
        grads[pl.ds(base, 512), :] = mm_tn(act[c], dff[...]).astype(BF)
        put(wf, c, 4, mm_tn(fin[...], dpre[c]))
        return 0

    for c in range(4):
        wgrad(c, 0)
    take(wf, 4, grads, ROW_UP - ROW_O)
    for j in range(PAIRS):
        grads[128 * j:128 * j + 128, :] = mm_tn(attended[j], dbr[...]).astype(BF)


def middle(lens, resid0, attended, cot, w):
    S = jax.ShapeDtypeStruct
    V = pltpu.VMEM
    return pl.pallas_call(
        mid_body,
        out_shape=[S((T, D), BF), S((T, D), F32), S((PAIRS, T, 128), BF), S((ROW_T - ROW_O, D), BF), S((8, D), F32)],
        in_specs=[sm()] + [vm()] * 4, out_specs=[vm()] * 5,
        scratch_shapes=[V((4, 2048, 128), F32), V((4, D, D), BF), V((4, T, D), BF), V((4, T, D), BF), V((T, D), BF), V((T, D), BF), V((T, D), BF)],
        compiler_params=pltpu.CompilerParams(vmem_limit_bytes=VMEM_LIMIT),
        name="middle",
    )(lens, resid0, attended, cot, w)


def bwd_body(lens, qkv, lse, datt, attn_in, resid0, dres, ids, feat, w, small, gin, ga, gt, dqkv, accv, wf, wq, slots, cacc):
    unpack(w, 0, 3, wf, wq)
    vecs = w[ROW_C + 16:ROW_C + TAIL, :].astype(F32)
    o = ROW_V - ROW_C - 16
    g1 = vecs[o:o + 1]
    long = lens[0, 1] == 0

    def attend(i, _):
        pair, qb = lax.div(i, NB), lax.rem(i, NB)
        rows = pl.ds(pl.multiple_of(qb * BLK, BLK), BLK)
        q = qkv[pair, rows, :] * jnp.asarray(SCALE, BF)
        k = qkv[PAIRS + pair]
        v = qkv[2 * PAIRS + pair]
        do = datt[pair, rows, :]
        bias = key_bias(lens, qb)
        dqs = []

        @pl.when(qb == 0)
        def _():
            accv[...] = jnp.zeros_like(accv)

        for par in (0, 1):
            half = lane_half(par)
            qm = jnp.where(half, q, jnp.zeros_like(q))
            dm = jnp.where(half, do, jnp.zeros_like(do))
            p = jnp.exp(mm_nt(k, qm) + bias - lse[pl.ds(2 * pair + par, 1), rows])
            dp = mm_nt(v, dm)
            delta = jnp.sum(p * dp, axis=0, keepdims=True)
            ds = (p * (dp - delta)).astype(BF)
            accv[1] += mm(p.astype(BF), dm)
            accv[0] += mm(ds, qm)
            dqs.append(mm_tn(ds, k))
        dqkv[pair, rows, :] = (jnp.where(lane_half(0), dqs[0], dqs[1]) * SCALE).astype(BF)

        @pl.when(qb == NB - 1)
        def _():
            dqkv[PAIRS + pair] = accv[0].astype(BF)
            dqkv[2 * PAIRS + pair] = accv[1].astype(BF)
        return 0

    lax.fori_loop(0, PAIRS * NB, attend, 0)

    cols = []
    for c in range(3):
        dq = jnp.concatenate([dqkv[4 * c + j] for j in range(4)], axis=1)
        put(wf, c, 3, mm_tn(attn_in[...], dq))
        if c != 1:
            cols.append(jnp.sum(dq.astype(F32), axis=0, keepdims=True))
    take(wf, 3, ga, 0)
    slots[...] = jnp.zeros_like(slots)
    cacc[...] = jnp.zeros_like(cacc)

    def block(b, _):
        rows = pl.ds(pl.multiple_of(b * BLK, BLK), BLK)
        e1 = jnp.zeros((BLK, D), F32)
        for c in range(3):
            dq = jnp.concatenate([dqkv[4 * c + j, rows, :] for j in range(4)], axis=1)
            e1 = e1 + mm_nt(dq, wq[c])
        n, inv = norm(resid0[rows, :])
        slots[8:9, :] += jnp.sum(e1 * n, axis=0, keepdims=True)
        slots[9:10, :] += jnp.sum(e1, axis=0, keepdims=True)
        g = dres[rows, :] + norm_back(e1 * g1, n, inv)
        gin[rows, :] = g
        ds = g.astype(BF)
        oh = (lax.broadcasted_iota(jnp.int32, (32, BLK), 0) == ids[0:1, rows]).astype(F32).astype(BF)
        cacc[0:32, :] += mm(oh, ds)
        slot = jnp.where(long, 0, b)
        slots[pl.ds(slot, 1), :] += jnp.sum(ds.astype(F32), axis=0, keepdims=True)
        return 0

    lax.fori_loop(0, NB, block, 0)
    f = feat[...].astype(F32)
    gt[0:256, :] = lax.dot_general(f, slots[0:8, :], (((0,), (0,)), ((), ())), precision=lax.Precision.HIGHEST, preferred_element_type=F32).astype(BF)
    o = ROW_V - ROW_C
    cacc[o:o + 2, :] = slots[8:10, :]
    cacc[o + 2:o + 4, :] = small[1:3, :]
    cacc[o + 4:o + 5, :] = cols[0]
    cacc[o + 5:o + 6, :] = cols[1]
    cacc[o + 6:o + 7, :] = small[3:4, :]
    cacc[o + 7:o + 8, :] = small[0:1, :]
    cacc[o + 8:o + 12, :] = small[4:8, :]
    gt[256:256 + TAIL, :] = cacc[...].astype(BF)


def backward(lens, qkv, lse, datt, attn_in, resid0, dres, ids, feat, w, small):
    S = jax.ShapeDtypeStruct
    V = pltpu.VMEM
    return pl.pallas_call(
        bwd_body,
        out_shape=[S((T, D), F32), S((ROW_O, D), BF), S((256 + TAIL, D), BF)],
        in_specs=[sm()] + [vm()] * 10, out_specs=[vm()] * 3,
        scratch_shapes=[V((12, T, 128), BF), V((2, T, 128), F32), V((4, 1536, 128), F32), V((3, D, D), BF), V((16, D), F32), V((TAIL, D), F32)],
        compiler_params=pltpu.CompilerParams(vmem_limit_bytes=VMEM_LIMIT),
        name="backward",
    )(lens, qkv, lse, datt, attn_in, resid0, dres, ids, feat, w, small)


def time_features(steps):
    half = 128
    freqs = jnp.exp(-math.log(10000.0) * jnp.arange(half, dtype=F32) / half)
    ang = steps.astype(F32).reshape(4, 1) * freqs
    f = jnp.concatenate([jnp.sin(ang), jnp.cos(ang)], axis=-1).astype(BF)
    return jnp.pad(f, ((0, 4), (0, 0)))


def step(inputs, ids, timesteps, lens, cot, w):
    x = inputs.reshape(T, D)
    feat = time_features(timesteps)
    resid0, attn_in, qkv, attended, lse = forward(lens, x, ids, feat, w)
    out, dres, datt, gmid, small = middle(lens, resid0, attended, cot.reshape(T, D), w)
    gin, ga, gt = backward(lens, qkv, lse, datt, attn_in, resid0, dres, ids, feat, w, small)
    return out, gin, ga, gmid, gt


def offset_in_chunk(plan, nfs):
    i = lax.axis_index("dp") * nfs + lax.axis_index("fsdp")
    return i * plan.share - lax.div(i * plan.share, ROW * TILE) * (TILE * ROW)


def shards(inputs, noisy_ids, timesteps, doc_lens, cotangent, params, momentum, average):
    ndp, nfs = lax.axis_size("dp"), lax.axis_size("fsdp")
    device_count = ndp * nfs
    row_count, seq_len, model_width = inputs.shape
    plan = Plan(ndp, nfs, params.shape[0] * device_count)
    offset = offset_in_chunk(plan, nfs)
    chunk = lax.dynamic_update_slice(
        jnp.zeros((plan.rows * ROW,), BF), params.astype(BF), (offset,)
    ).reshape(plan.rows, ROW)
    weights = gather_all(plan, chunk, 0)
    output, input_grad, ga, gmid, gt = step(
        inputs, noisy_ids, timesteps, doc_lens, cotangent, weights
    )
    rows = jnp.concatenate([ga, gmid, gt], axis=0)
    if plan.padded > rows.shape[0]:
        rows = jnp.pad(rows, ((0, plan.padded - rows.shape[0]), (0, 0)))
    owned = reduce_all(plan, rows[: plan.padded], 1)
    owned_grad = lax.dynamic_slice(owned.reshape(-1), (offset,), (plan.share,))
    gradient = owned_grad * (1.0 / math.sqrt(row_count * seq_len * device_count))
    new_momentum = MOMENTUM_RATE * momentum + gradient
    new_params = params - LEARN_RATE * (gradient + MOMENTUM_RATE * new_momentum)
    new_average = AVERAGE_RATE * average + (1.0 - AVERAGE_RATE) * new_params
    return (
        output.reshape(row_count, seq_len, model_width),
        input_grad.reshape(row_count, seq_len, model_width),
        new_params,
        new_momentum,
        new_average,
        new_params.astype(BF),
    )


def solution(mesh):
    rows = ("dp", "fsdp")
    in_specs = (
        P(rows, None, None),
        P(rows, None),
        P(rows, None),
        P(rows, None),
        P(rows, None, None),
        P(rows),
        P(rows),
        P(rows),
    )
    out_specs = (P(rows, None, None), P(rows, None, None), P(rows), P(rows), P(rows), P(rows))
    return jax.shard_map(shards, mesh=mesh, in_specs=in_specs, out_specs=out_specs, check_vma=False)
```

profile of v0, /device:TPU:0, one launch (start us, length us, event | category | flops | bytes accessed | tf_op | source)
XLA Modules:
  0.0 242.2 jit_solution(3565859018296042161)
XLA Ops:
  0.6 0.7 convert_bitcast_fusion
  1.3 0.1 fusion.3
  1.4 0.6 fusion.2.feat
  2.0 1.0 convert_element_type.13
  3.1 2.1 dynamic_update_slice.3
  5.2 0.8 reshape.38.chunk_ref
  6.0 61.4 %gather_all.1.w = bf16[6448,512]{1,0:T(8,128)(2,1)} custom-call(bf16[224,512]{1,0:T(8,128)(2,1)} %reshape.38.chunk_ref), custom_call_target="tpu_custom_call" | custom-call | tf_op jit(solution)/shard_map/gather_all/pallas_call | solution.py:213
  67.4 31.2 %forward.1 = (f32[1024,512]{1,0:T(8,128)}, bf16[1024,512]{1,0:T(8,128)(2,1)}, bf16[12,1024,128]{2,1,0:T(8,128)(2,1)}, bf16[4,1024,128]{2,1,0:T(8,128)(2,1)}, f32[8,1024]{1,0:T(8,128)}) custom-call(s32[1,4]{1,0:T(1,128)} %lens.5, bf16[1024,512]{1,0:T(8,128)(2,1)} %bitcast.10, s32[1,1024]{1,0:T(1,128)} %ids.3, bf16[8,256]{1,0:T(8,128)(2,1)} %fusion.2.feat, ...), custom_call_target="tpu_custom_call" | custom-call | tf_op jit(solution)/shard_map/forward/pallas_call | solution.py:472
  98.6 27.9 %middle.1 = (bf16[1024,512]{1,0:T(8,128)(2,1)}, f32[1024,512]{1,0:T(8,128)}, bf16[4,1024,128]{2,1,0:T(8,128)(2,1)}, bf16[4608,512]{1,0:T(8,128)(2,1)}, f32[8,512]{1,0:T(8,128)}) custom-call(s32[1,4]{1,0:T(1,128)} %lens.5, f32[1024,512]{1,0:T(8,128)} %get-tuple-element.19.resid0, bf16[4,1024,128]{2,1,0:T(8,128)(2,1)} %get-tuple-element.20.attended, ...), custom_call_target="tpu_custom_call" | custom-call | tf_op jit(solution)/shard_map/middle/pallas_call | solution.py:551
  126.5 49.6 %backward.1 = (f32[1024,512]{1,0:T(8,128)}, bf16[1536,512]{1,0:T(8,128)(2,1)}, bf16[304,512]{1,0:T(8,128)(2,1)}) custom-call(s32[1,4]{1,0:T(1,128)} %lens.5, bf16[12,1024,128]{2,1,0:T(8,128)(2,1)} %get-tuple-element.22.qkv, f32[8,1024]{1,0:T(8,128)} %get-tuple-element.23.lse, bf16[4,1024,128]{2,1,0:T(8,128)(2,1)} %get-tuple-element.24.datt, ...), custom_call_target="tpu_custom_call" | custom-call | tf_op jit(solution)/shard_map/backward/pallas_call | solution.py:648
  176.2 6.0 %pad_maximum_fusion.src_ref = bf16[6448,512]{1,0:T(8,128)(2,1)} fusion(bf16[304,512]{1,0:T(8,128)(2,1)} %get-tuple-element.31, bf16[4608,512]{1,0:T(8,128)(2,1)} %get-tuple-element.30, bf16[1536,512]{1,0:T(8,128)(2,1)} %get-tuple-element.29), kind=kLoop, calls=%fused_computation | loop fusion | flops 19808256 | bytes 13205504 | tf_op jit(solution)/shard_map/concatenate | solution.py:693
  182.2 0.0 copy-start
  182.2 0.0 copy-start.3
  182.2 0.0 copy-start.2
  182.2 56.9 %reduce_all.1 = f32[224,512]{1,0:T(8,128)} custom-call(bf16[6448,512]{1,0:T(8,128)(2,1)} %pad_maximum_fusion.src_ref), custom_call_target="tpu_custom_call" | custom-call | tf_op jit(solution)/shard_map/reduce_all/pallas_call | solution.py:323
  239.1 1.1 copy.14
  240.2 0.0 copy-done
  240.2 0.0 copy-done.3
  240.3 1.0 fusion.5
  241.3 0.0 copy-start.1
  241.3 0.0 copy-done.2
  241.3 0.9 multiply_add_fusion
  242.2 0.0 copy-done.1
  (2 shorter events, 0.0 us)
Async XLA Ops:
  182.2 58.0 %copy-start = (f32[103024]{0:T(1024)S(1)}, f32[103024]{0:T(1024)}, u32[]{:S(2)}) copy-start(f32[103024]{0:T(1024)} %param.13) | copy-start | bytes 1236292
  182.2 58.0 %copy-start.3 = (f32[103024]{0:T(1024)S(1)}, f32[103024]{0:T(1024)}, u32[]{:S(2)}) copy-start(f32[103024]{0:T(1024)} %param.14) | copy-start | bytes 1236292
  182.2 59.1 %copy-start.2 = (f32[103024]{0:T(1024)S(1)}, f32[103024]{0:T(1024)}, u32[]{:S(2)}) copy-start(f32[103024]{0:T(1024)} %param.15) | copy-start | bytes 1236292
  241.3 0.9 copy-start.1
where the time goes:
time: 242 us
  Pallas kernels  227 us (94%)
  other arithmetic  10.4 us (4%)
  local copies, waits for them, and re-layouts  4.07 us (2%)
    pallas_call x1, Pallas kernels, gather_all(): pl.pallas_call(kern, out_shape=jax.ShapeDtypeStruct((plan.padded, ROW), B...  61.4 us
    pallas_call x1, Pallas kernels, reduce_all(): pl.pallas_call(kern, out_shape=jax.ShapeDtypeStruct((n, ROW), F32), in_sp...  56.9 us
    pallas_call x1, Pallas kernels, backward(): pl.pallas_call(bwd_body, out_shape=[S((T, D), F32), S((ROW_O, D), BF), S(...  49.6 us
    pallas_call x1, Pallas kernels, forward(): pl.pallas_call(fwd_body, out_shape=[S((T, D), F32), S((T, D), BF), S((12,...  31.2 us
    pallas_call x1, Pallas kernels, middle(): pl.pallas_call(mid_body, out_shape=[S((T, D), BF), S((T, D), F32), S((PAI...  27.9 us
    concatenate x1, other arithmetic, shards(): rows = jnp.concatenate([ga, gmid, gt], axis=0)  6.04 us

commit v1 on v0

v1 whole, which is shorter than its diff:
```python
import math

import jax
import jax.numpy as jnp
from jax import lax
from jax.experimental import pallas as pl
from jax.experimental.pallas import tpu as pltpu
from jax.sharding import PartitionSpec as P

MOMENTUM_RATE = 0.9
LEARN_RATE = 0.02
AVERAGE_RATE = 0.8
EPSILON = 1e-5
MESH = pl.DeviceIdType.MESH
BF = jnp.bfloat16
F32 = jnp.float32
ROW = 512
TILE = 16
T = 1024
D = 512
BLK = 256
NB = T // BLK
PAIRS = 4
SCALE = 0.125
ROW_O, ROW_UP, ROW_DOWN, ROW_T, ROW_C, ROW_V = 1536, 2048, 4096, 6144, 6400, 6427
TAIL = 48
AG_KINDS = 13
RS_KINDS = 6
HOOKS = NB + PAIRS * NB


class Plan:
    def __init__(self, ndp, nfs, total):
        self.nx, self.ny, self.nc = 2, 2, nfs // 2
        self.nz = ndp // 2
        self.count = ndp * nfs
        self.share = total // self.count
        self.starts = [((i * self.share) // (ROW * TILE)) * TILE for i in range(self.count)]
        ends = [-(-((i + 1) * self.share) // ROW) for i in range(self.count)]
        need = max(e - s for e, s in zip(ends, self.starts))
        self.rows = max(2, -(-need // TILE)) * TILE
        self.half = -(-self.rows // (2 * TILE)) * TILE
        self.padded = max(max(self.starts) + self.rows, ROW_C + TAIL)
        layer = self.count // self.nz
        last = self.nz - 1
        self.lo = next(r for r in range(self.nz) if self.starts[r * layer] >= ROW_O)
        first = next(i for i in range(self.count) if self.starts[i] + self.rows > ROW_T)
        self.only = first >= self.count - self.nc
        self.hi = last if self.only else first // layer - 1
        self.early = list(range(self.lo)) + list(range(last if self.only else self.hi + 1, self.nz))
        self.late = list(range(self.lo, self.hi + 1))

    def early_pick(self, r, cx, cy):
        if self.only and r == self.nz - 1:
            return cx * cy == 1
        return True

    def late_pick(self, r, cx, cy):
        if self.only and r == self.nz - 1:
            return cx * cy == 0
        return True


class Place:
    def __init__(self, plan):
        d = lax.axis_index("dp")
        f = lax.axis_index("fsdp")
        self.plan = plan
        two = jnp.int32(2)
        self.z, self.x = lax.div(d, two), lax.rem(d, two)
        self.y, self.c = lax.div(f, two), lax.rem(f, two)
        self.X = self.dev(x=1 - self.x)
        self.Y = self.dev(y=1 - self.y)
        self.C = self.dev(c=1 - self.c)

    def dev(self, z=None, x=None, y=None, c=None):
        z = self.z if z is None else z
        x = self.x if x is None else x
        y = self.y if y is None else y
        c = self.c if c is None else c
        return (z * 2 + x, y * 2 + c)

    def partners(self):
        nz = self.plan.nz
        others = [self.dev(z=lax.rem(self.z + s, jnp.int32(nz))) for s in range(1, nz)]
        return [self.X, self.Y, self.C] + others

    def far(self, r):
        return jnp.abs(self.z - r)


def signal_all(place, sem):
    for dev in place.partners():
        pl.semaphore_signal(sem, inc=1, device_id=dev, device_id_type=MESH)


def wait_all(place, sem):
    pl.semaphore_wait(sem, 3 + place.plan.nz - 1)


def rcopy(src, dst, ss, rs, dev):
    return pltpu.make_async_remote_copy(
        src_ref=src, dst_ref=dst, send_sem=ss, recv_sem=rs, device_id=dev, device_id_type=MESH
    )


def when(*conds):
    real = [c for c in conds if c is not True]

    def run(f):
        if not real:
            return f()
        c = real[0]
        for other in real[1:]:
            c = c & other
        return pl.when(c)(f)

    return run


class Gather:
    def __init__(self, p, g, zs, zr, ps, pr):
        self.p, self.g, self.zs, self.zr, self.ps, self.pr = p, g, zs, zr, ps, pr
        h, n = p.plan.half, p.plan.rows
        self.parts = (pl.ds(0, h), pl.ds(h, n - h), pl.ds(0, n))

    def zcopy(self, r, j, up):
        p = self.p
        ref = self.g.at[r, p.x, p.y, p.c, self.parts[j]]
        return rcopy(ref, ref, self.zs.at[r, j, 0 if up else 1], self.zr.at[r, j], p.dev(z=p.z + 1 if up else p.z - 1))

    def cp(self, r, k):
        p = self.p
        a, b, w = self.parts
        x, y = p.x, p.y
        cx, cy, part, dev = (
            (x, y, a, p.X), (x, y, b, p.Y), (x, y, a, p.Y), (x, y, b, p.X),
            (1 - x, y, a, p.Y), (x, 1 - y, b, p.X), (x, y, w, p.C), (1 - x, y, a, p.C), (x, 1 - y, b, p.C),
            (x, 1 - y, a, p.C), (1 - x, 1 - y, a, p.C), (1 - x, y, b, p.C), (1 - x, 1 - y, b, p.C),
        )[k]
        ref = self.g.at[r, cx, cy, p.c, part]
        return rcopy(ref, ref, self.ps.at[r, k], self.pr.at[r, k], dev)

    def stage(self, s, r, pick):
        p = self.p
        z, x, y, nz = p.z, p.x, p.y, p.plan.nz
        if s == 0:
            for j in (0, 1):
                if r < nz - 1:
                    when(z == r, pick(r, x, y))(lambda: self.zcopy(r, j, True).start())
                if r > 0:
                    when(z == r, pick(r, x, y))(lambda: self.zcopy(r, j, False).start())
        if s == 1:
            for j in (0, 1):
                when(z != r, pick(r, x, y))(lambda: self.zcopy(r, j, True).wait_recv())
                if 0 < r < nz - 1 or r == 0:
                    when(z > r, z < nz - 1, pick(r, x, y))(lambda: self.zcopy(r, j, True).start())
                if r > 0:
                    when(z < r, z > 0, pick(r, x, y))(lambda: self.zcopy(r, j, False).start())
                when(pick(r, x, y))(lambda: self.cp(r, j).start())

            def rest():
                for k in (2, 3, 6):
                    self.cp(r, k).start()

            when(pick(r, x, y))(rest)
        if s == 2:
            for k, a, b, cx, cy in ((0, 4, 7, 1 - x, y), (1, 5, 8, x, 1 - y)):
                def go():
                    self.cp(r, k).wait_recv()
                    self.cp(r, a).start()
                    self.cp(r, b).start()

                when(pick(r, cx, cy))(go)
        if s == 3:
            for k, a, cx, cy in ((2, 9, x, 1 - y), (4, 10, 1 - x, 1 - y), (3, 11, 1 - x, y), (5, 12, 1 - x, 1 - y)):
                def go():
                    self.cp(r, k).wait_recv()
                    self.cp(r, a).start()

                when(pick(r, cx, cy))(go)
        if s == 4:
            for ks, cx, cy in (((6,), x, y), ((7, 11), 1 - x, y), ((8, 9), x, 1 - y), ((10, 12), 1 - x, 1 - y)):
                def go():
                    for k in ks:
                        self.cp(r, k).wait_recv()

                when(pick(r, cx, cy))(go)

    def drain(self):
        z, nz = self.p.z, self.p.plan.nz
        for r in range(nz):
            for j in (0, 1):
                if r < nz - 1:
                    when(z >= r, z < nz - 1)(lambda: self.zcopy(r, j, True).wait_send())
                if r > 0:
                    when(z <= r, z > 0)(lambda: self.zcopy(r, j, False).wait_send())
            for k in range(AG_KINDS):
                self.cp(r, k).wait_send()


class Reduce:
    def __init__(self, p, src, g, cs, cr, ps, pr, zs, zr):
        self.p, self.src, self.g = p, src, g
        self.cs, self.cr, self.ps, self.pr, self.zs, self.zr = cs, cr, ps, pr, zs, zr
        self.h, self.n = p.plan.half, p.plan.rows
        self.a, self.b = pl.ds(0, self.h), pl.ds(self.h, self.n - self.h)

    def rows(self, r, xx, yy, cc):
        plan = self.p.plan
        i = ((r * 2 + xx) * 2 + yy) * 2 + cc
        return pl.ds(pl.multiple_of(lax.div(i * plan.share, jnp.int32(ROW * TILE)) * TILE, TILE), self.n)

    def cb(self, r, xx, yy, *rest):
        return self.g.at[(r, xx, yy, 0) + rest]

    def pa(self, r, xx):
        return self.g.at[r, 0, xx, 1, self.a]

    def pb(self, r, yy):
        return self.g.at[r, 0, yy, 1, self.b]

    def p2(self, r, *rest):
        return self.g.at[(r, 1, 0, 1) + rest]

    def zb(self, s):
        return self.g.at[s, 1, 1, 1]

    def ccopy(self, r, xx, yy):
        p = self.p
        return rcopy(
            self.src.at[self.rows(r, xx, yy, 1 - p.c)], self.cb(r, xx, yy),
            self.cs.at[r, xx, yy], self.cr.at[r, xx, yy], p.C,
        )

    def cp(self, r, k):
        p = self.p
        x, y = p.x, p.y
        s, d, dev = (
            (self.cb(r, 0, 1 - y, self.a), self.pa(r, 0), p.Y),
            (self.cb(r, 1, 1 - y, self.a), self.pa(r, 1), p.Y),
            (self.cb(r, 1 - x, 0, self.b), self.pb(r, 0), p.X),
            (self.cb(r, 1 - x, 1, self.b), self.pb(r, 1), p.X),
            (self.pa(r, 1 - x), self.p2(r, self.a), p.X),
            (self.pb(r, 1 - y), self.p2(r, self.b), p.Y),
        )[k]
        return rcopy(s, d, self.ps.at[r, k], self.pr.at[r, k], dev)

    def zcopy(self, r):
        p = self.p
        return rcopy(self.p2(r), self.zb(p.z), self.zs.at[r], self.zr.at[p.z], p.dev(z=r))

    def zwait(self, s):
        rcopy(self.p2(0), self.zb(s), self.zs.at[0], self.zr.at[s], self.p.dev(z=s)).wait_recv()

    def stage(self, s, r, pick):
        p = self.p
        z, x, y = p.z, p.x, p.y
        both = [(xx, yy) for xx in (0, 1) for yy in (0, 1)]
        if s == 0:
            for xx, yy in both:
                when(pick(r, xx, yy))(lambda: self.ccopy(r, xx, yy).start())
        if s == 1:
            for xx, yy in both:
                def go():
                    self.ccopy(r, xx, yy).wait_recv()
                    ref = self.cb(r, xx, yy)
                    ref[...] = ref[...] + self.src[self.rows(r, xx, yy, p.c), :]

                when(pick(r, xx, yy))(go)
            for q in (0, 1):
                when(pick(r, q, 1 - y))(lambda: self.cp(r, q).start())
                when(pick(r, 1 - x, q))(lambda: self.cp(r, 2 + q).start())
        if s == 2:
            for q in (0, 1):
                def goa():
                    self.cp(r, q).wait_recv()
                    ref = self.pa(r, q)
                    ref[...] = ref[...] + self.cb(r, q, y, self.a)[...]

                when(pick(r, q, y))(goa)
            when(pick(r, 1 - x, y))(lambda: self.cp(r, 4).start())
            for q in (0, 1):
                def gob():
                    self.cp(r, 2 + q).wait_recv()
                    ref = self.pb(r, q)
                    ref[...] = ref[...] + self.cb(r, x, q, self.b)[...]

                when(pick(r, x, q))(gob)
            when(pick(r, x, 1 - y))(lambda: self.cp(r, 5).start())
        if s == 3:
            def fin():
                self.cp(r, 4).wait_recv()
                ref = self.p2(r, self.a)
                ref[...] = ref[...] + self.pa(r, x)[...]
                self.cp(r, 5).wait_recv()
                ref = self.p2(r, self.b)
                ref[...] = ref[...] + self.pb(r, y)[...]

            when(pick(r, x, y))(fin)
            when(pick(r, x, y), z != r)(lambda: self.zcopy(r).start())

    def finish(self, out):
        z = self.p.z
        out[...] = self.p2(z)[...].astype(F32)
        for s in range(self.p.plan.nz):
            def go():
                self.zwait(s)
                out[...] += self.zb(s)[...].astype(F32)

            when(z != s)(go)

    def drain(self):
        for r in range(self.p.plan.nz):
            for xx in (0, 1):
                for yy in (0, 1):
                    self.ccopy(r, xx, yy).wait_send()
            for k in range(RS_KINDS):
                self.cp(r, k).wait_send()
            when(self.p.z != r)(lambda: self.zcopy(r).wait_send())


def pipelined(stages, layers):
    order = []
    for t in range(len(layers) + len(stages) - 1):
        for s in reversed(range(len(stages))):
            if 0 <= t - s < len(layers):
                order.append((stages[s], layers[t - s]))
    return order


def assemble(plan, g, lo, hi, store):
    for i in range(plan.count):
        at = lambda k: (k // 8, (k // 4) % 2, (k // 2) % 2, k % 2)
        s = plan.starts[i]
        e = plan.starts[i + 1] if i + 1 < plan.count else plan.padded
        if lo <= s < hi:
            head = g[at(i) + (slice(0, TILE),)]
            if i and s - plan.starts[i - 1] < plan.rows:
                d = s - plan.starts[i - 1]
                head = head + g[at(i - 1) + (slice(d, d + TILE),)]
            store(s, s + TILE, head)
        a, b = max(s + TILE, lo), min(e, hi, s + plan.rows)
        if b > a:
            store(a, b, g[at(i) + (slice(a - s, b - s),)])


def mm(a, b):
    return lax.dot_general(a, b, (((1,), (0,)), ((), ())), preferred_element_type=F32)


def mm_nt(a, b):
    return lax.dot_general(a, b, (((1,), (1,)), ((), ())), preferred_element_type=F32)


def mm_tn(a, b):
    return lax.dot_general(a, b, (((0,), (0,)), ((), ())), preferred_element_type=F32)


def norm(h):
    mean = jnp.mean(h, axis=-1, keepdims=True)
    cen = h - mean
    inv = lax.rsqrt(jnp.mean(cen * cen, axis=-1, keepdims=True) + EPSILON)
    return cen * inv, inv


def norm_back(dn, n, inv):
    return (dn - jnp.mean(dn, axis=-1, keepdims=True) - n * jnp.mean(dn * n, axis=-1, keepdims=True)) * inv


def valid_len(lens, b):
    long = lens[0, 1] == 0
    short = lens[0, 0]
    for k in range(1, NB):
        short = jnp.where(b == k, lens[0, k], short)
    return jnp.where(long, lens[0, 0] - b * BLK, short)


def lane_half(par):
    lane = lax.broadcasted_iota(jnp.int32, (1, 128), 1)
    return (lane >= 64) if par else (lane < 64)


def key_bias(lens, qb):
    long = lens[0, 1] == 0
    cols = []
    it = lax.broadcasted_iota(jnp.int32, (BLK, 1), 0)
    for kb in range(NB):
        thr = jnp.where(long | (qb == kb), valid_len(lens, kb), 0)
        cols.append(jnp.where(it < thr, 0.0, -1e30).astype(F32))
    return jnp.concatenate(cols, axis=0)


def lanes(j):
    return slice(128 * j, 128 * j + 128)


def spread(wf, base):
    def store(a, b, val):
        for j in range(4):
            wf[j, a - base:b - base, :] = val[:, lanes(j)].astype(F32)
    return store


def regroup(wf, n, to):
    for c in range(n):
        for j in range(4):
            to[c, :, lanes(j)] = wf[j, pl.ds(c, 512, stride=n), :].astype(BF)


def put(wf, c, n, val):
    for j in range(4):
        wf[j, pl.ds(c, 512, stride=n), :] = val[:, lanes(j)]


def take(wf, n, out, base):
    for j in range(4):
        out[base:base + 512 * n, lanes(j)] = wf[j, 0:512 * n, :].astype(BF)


def phi_parts(v):
    cdf = 0.5 * (1.0 + lax.erf(v * (2.0 ** -0.5)))
    pdf = jnp.exp(v * v * -0.5) * (1.0 / math.sqrt(2.0 * math.pi))
    return cdf, pdf


def block_rows(b):
    return pl.ds(pl.multiple_of(b * BLK, BLK), BLK)


def body(plan, lens, ids, feat, x_hbm, cot_hbm, chunk_hbm, out_hbm, gin_hbm, own,
         g, src, wf, wq, wu, wo, wd, vec, xs, cs, resid0, attn_in, qkv, attended, lse, ft,
         act, dpre, fin, dff, dbr, dres, datt, dqkv, accv, slots, small, cacc,
         zs, zr, ps, pr, rcs, rcr, rps, rpr, rzs, rzr, ready, ins, outs, gins):
    p = Place(plan)
    nz = plan.nz
    gather = Gather(p, g, zs, zr, ps, pr)
    loads = [
        pltpu.make_async_copy(chunk_hbm, g.at[p.z, p.x, p.y, p.c], ins.at[0]),
        pltpu.make_async_copy(x_hbm, xs, ins.at[1]),
        pltpu.make_async_copy(cot_hbm, cs, ins.at[2]),
    ]
    for cpy in loads:
        cpy.start()
    bar = pltpu.get_barrier_semaphore()
    signal_all(p, bar)
    wait_all(p, bar)
    loads[0].wait()

    for r in plan.early:
        gather.stage(0, r, plan.early_pick)
    for t in range(nz + 3):
        for s in (4, 3, 2, 1):
            for r in plan.early:
                if 0 <= t - (s - 1) < nz:
                    when(p.far(r) == t - (s - 1))(lambda: gather.stage(s, r, plan.early_pick))
    for r in plan.late:
        gather.stage(0, r, plan.late_pick)

    def gather_hook(i):
        for s in (1, 2, 3, 4):
            for r in plan.late:
                start = lax.div(9 * p.far(r) + 2, jnp.int32(2)) + (0, 0, 3, 6, 7)[s]
                when(i == jnp.minimum(start, HOOKS))(lambda: gather.stage(s, r, plan.late_pick))

    assemble(plan, g, 0, ROW_O, spread(wf, 0))
    regroup(wf, 3, wq)

    def tail_store(a, b, val):
        vec[a - ROW_T:b - ROW_T, :] = val

    assemble(plan, g, ROW_T, ROW_C + TAIL, tail_store)
    ctab = vec[256:288, :]
    vecs = vec[272:304, :].astype(F32)
    v0 = ROW_V - ROW_C - 16
    g1, b1, g2, b2, bq, bv, bo, bd = (vecs[v0 + k:v0 + k + 1] for k in range(8))
    ft[...] = mm(feat[...], vec[0:256, :])
    long = lens[0, 1] == 0
    loads[1].wait()

    def embed(b, _):
        gather_hook(b)
        rows = block_rows(b)
        oh = (lax.broadcasted_iota(jnp.int32, (32, BLK), 0) == ids[0:1, rows]).astype(F32).astype(BF)
        side = mm_tn(oh, ctab)
        slot = jnp.where(long, 0, b)
        h = xs[rows, :].astype(F32) + (side + ft[pl.ds(slot, 1), :])
        resid0[rows, :] = h
        n, _i = norm(h)
        a = (n * g1 + b1).astype(BF)
        attn_in[rows, :] = a
        for c in range(3):
            pr_ = mm(a, wq[c])
            if c == 0:
                pr_ = pr_ + bq
            if c == 2:
                pr_ = pr_ + bv
            pr_ = pr_.astype(BF)
            for j in range(4):
                qkv[4 * c + j, rows, :] = pr_[:, lanes(j)]
        return 0

    lax.fori_loop(0, NB, embed, 0)
    ones = jnp.ones((T, 128), BF)

    def attend(i, _):
        gather_hook(i + NB)
        pair, qb = lax.div(i, NB), lax.rem(i, NB)
        rows = block_rows(qb)
        q = qkv[pair, rows, :] * jnp.asarray(SCALE, BF)
        k = qkv[PAIRS + pair]
        va = jnp.concatenate([qkv[2 * PAIRS + pair], ones], axis=1)
        bias = key_bias(lens, qb)
        heads = []
        for par in (0, 1):
            qm = jnp.where(lane_half(par), q, jnp.zeros_like(q))
            s = mm_nt(k, qm) + bias
            m = jnp.max(s, axis=0, keepdims=True)
            e = jnp.exp(s - m)
            l = jnp.sum(e, axis=0, keepdims=True)
            lse[pl.ds(2 * pair + par, 1), rows] = m + jnp.log(l)
            oa = mm_tn(e.astype(BF), va)
            heads.append(oa[:, :128] / oa[:, 128:])
        attended[pair, rows, :] = jnp.where(lane_half(0), heads[0], heads[1]).astype(BF)
        return 0

    lax.fori_loop(0, PAIRS * NB, attend, 0)
    gather_hook(HOOKS)

    def wo_store(a, b, val):
        wo[a - ROW_O:b - ROW_O, :] = val

    def wd_store(a, b, val):
        wd[a - ROW_DOWN:b - ROW_DOWN, :] = val

    assemble(plan, g, ROW_O, ROW_UP, wo_store)
    assemble(plan, g, ROW_UP, ROW_DOWN, spread(wf, ROW_UP))
    assemble(plan, g, ROW_DOWN, ROW_T, wd_store)
    regroup(wf, 4, wu)
    gather.drain()
    signal_all(p, ready)
    small[...] = jnp.zeros_like(small)
    loads[2].wait()

    def feed(b, _):
        rows = block_rows(b)
        att = jnp.concatenate([attended[j, rows, :] for j in range(PAIRS)], axis=1)
        h = resid0[rows, :] + (mm(att, wo[...]) + bo)
        n, inv = norm(h)
        f = (n * g2 + b2).astype(BF)
        fin[rows, :] = f
        ok = lax.broadcasted_iota(jnp.int32, (BLK, 1), 0) < valid_len(lens, b)
        do = jnp.where(ok, cs[rows, :].astype(F32), 0.0)
        d = do.astype(BF)
        dff[rows, :] = d
        small[0:1, :] += jnp.sum(do, axis=0, keepdims=True)
        acc = h + bd
        e2 = jnp.zeros((BLK, D), F32)
        for c in range(4):
            pre = mm(f, wu[c]) + vecs[v0 + 8 + c:v0 + 9 + c]
            cdf, pdf = phi_parts(pre)
            a = (pre * cdf).astype(BF)
            wdc = wd[512 * c:512 * c + 512, :]
            dp = (mm_nt(d, wdc) * (cdf + pre * pdf)).astype(BF)
            act[c, rows, :] = a
            dpre[c, rows, :] = dp
            small[4 + c:5 + c, :] += jnp.sum(dp.astype(F32), axis=0, keepdims=True)
            acc = acc + mm(a, wdc)
            e2 = e2 + mm_nt(dp, wu[c])
        xs[rows, :] = acc.astype(BF)
        pltpu.make_async_copy(xs.at[rows], out_hbm.at[rows], outs.at[b]).start()
        small[1:2, :] += jnp.sum(e2 * n, axis=0, keepdims=True)
        small[2:3, :] += jnp.sum(e2, axis=0, keepdims=True)
        dr = do + norm_back(e2 * g2, n, inv)
        dres[rows, :] = dr
        db = dr.astype(BF)
        dbr[rows, :] = db
        small[3:4, :] += jnp.sum(db.astype(F32), axis=0, keepdims=True)
        da = mm_nt(db, wo[...]).astype(BF)
        for j in range(PAIRS):
            datt[j, rows, :] = da[:, lanes(j)]
        return 0

    lax.fori_loop(0, NB, feed, 0)
    for c in range(4):
        src[ROW_DOWN + 512 * c:ROW_DOWN + 512 * c + 512, :] = mm_tn(act[c], dff[...]).astype(BF)
        put(wf, c, 4, mm_tn(fin[...], dpre[c]))
    take(wf, 4, src, ROW_UP)
    for j in range(PAIRS):
        src[ROW_O + 128 * j:ROW_O + 128 * j + 128, :] = mm_tn(attended[j], dbr[...]).astype(BF)

    reduce = Reduce(p, src, g, rcs, rcr, rps, rpr, rzs, rzr)
    wait_all(p, ready)
    for r in plan.late:
        reduce.stage(0, r, plan.late_pick)

    def reduce_hook(i):
        for k, r in enumerate(plan.late):
            for s, at in ((1, 1 + 3 * k), (2, 4 + 3 * k), (3, 6 + 3 * k)):
                when(i == min(at, PAIRS * NB))(lambda: reduce.stage(s, r, plan.late_pick))

    def attend_back(i, _):
        reduce_hook(i)
        pair, qb = lax.div(i, NB), lax.rem(i, NB)
        rows = block_rows(qb)
        q = qkv[pair, rows, :] * jnp.asarray(SCALE, BF)
        k = qkv[PAIRS + pair]
        v = qkv[2 * PAIRS + pair]
        do = datt[pair, rows, :]
        bias = key_bias(lens, qb)
        dqs = []

        @pl.when(qb == 0)
        def _():
            accv[...] = jnp.zeros_like(accv)

        for par in (0, 1):
            half = lane_half(par)
            qm = jnp.where(half, q, jnp.zeros_like(q))
            dm = jnp.where(half, do, jnp.zeros_like(do))
            pp = jnp.exp(mm_nt(k, qm) + bias - lse[pl.ds(2 * pair + par, 1), rows])
            dp = mm_nt(v, dm)
            delta = jnp.sum(pp * dp, axis=0, keepdims=True)
            ds = (pp * (dp - delta)).astype(BF)
            accv[1] += mm(pp.astype(BF), dm)
            accv[0] += mm(ds, qm)
            dqs.append(mm_tn(ds, k))
        dqkv[pair, rows, :] = (jnp.where(lane_half(0), dqs[0], dqs[1]) * SCALE).astype(BF)

        @pl.when(qb == NB - 1)
        def _():
            dqkv[PAIRS + pair] = accv[0].astype(BF)
            dqkv[2 * PAIRS + pair] = accv[1].astype(BF)
        return 0

    lax.fori_loop(0, PAIRS * NB, attend_back, 0)
    reduce_hook(PAIRS * NB)

    cols = []
    for c in range(3):
        dq = jnp.concatenate([dqkv[4 * c + j] for j in range(4)], axis=1)
        put(wf, c, 3, mm_tn(attn_in[...], dq))
        if c != 1:
            cols.append(jnp.sum(dq.astype(F32), axis=0, keepdims=True))
    take(wf, 3, src, 0)
    heads = [r for r in plan.early if r < plan.lo]
    tails = [r for r in plan.early if r >= plan.lo]
    for r in heads:
        reduce.stage(0, r, plan.early_pick)
    slots[...] = jnp.zeros_like(slots)
    cacc[...] = jnp.zeros_like(cacc)

    def embed_back(b, _):
        rows = block_rows(b)

        @pl.when(b == 1)
        def _():
            for r in heads:
                reduce.stage(1, r, plan.early_pick)

        e1 = jnp.zeros((BLK, D), F32)
        for c in range(3):
            dq = jnp.concatenate([dqkv[4 * c + j, rows, :] for j in range(4)], axis=1)
            e1 = e1 + mm_nt(dq, wq[c])
        n, inv = norm(resid0[rows, :])
        slots[8:9, :] += jnp.sum(e1 * n, axis=0, keepdims=True)
        slots[9:10, :] += jnp.sum(e1, axis=0, keepdims=True)
        gi = dres[rows, :] + norm_back(e1 * g1, n, inv)
        resid0[rows, :] = gi
        pltpu.make_async_copy(resid0.at[rows], gin_hbm.at[rows], gins.at[b]).start()
        ds = gi.astype(BF)
        oh = (lax.broadcasted_iota(jnp.int32, (32, BLK), 0) == ids[0:1, rows]).astype(F32).astype(BF)
        cacc[0:32, :] += mm(oh, ds)
        slots[pl.ds(b, 1), :] = jnp.sum(ds.astype(F32), axis=0, keepdims=True)
        return 0

    lax.fori_loop(0, NB, embed_back, 0)
    per = slots[0:8, :]
    total = jnp.sum(per, axis=0, keepdims=True)
    first = lax.broadcasted_iota(jnp.int32, (8, 1), 0) == 0
    per = jnp.where(long, jnp.where(first, total, 0.0), per)
    src[ROW_T:ROW_C, :] = lax.dot_general(
        feat[...].astype(F32), per, (((0,), (0,)), ((), ())),
        precision=lax.Precision.HIGHEST, preferred_element_type=F32,
    ).astype(BF)
    o = ROW_V - ROW_C
    cacc[o:o + 2, :] = slots[8:10, :]
    cacc[o + 2:o + 4, :] = small[1:3, :]
    cacc[o + 4:o + 5, :] = cols[0]
    cacc[o + 5:o + 6, :] = cols[1]
    cacc[o + 6:o + 7, :] = small[3:4, :]
    cacc[o + 7:o + 8, :] = small[0:1, :]
    cacc[o + 8:o + 12, :] = small[4:8, :]
    src[ROW_C:ROW_C + TAIL, :] = cacc[...].astype(BF)
    if plan.padded > ROW_C + TAIL:
        src[ROW_C + TAIL:plan.padded, :] = jnp.zeros((plan.padded - ROW_C - TAIL, ROW), BF)

    for r in tails:
        reduce.stage(0, r, plan.early_pick)
    for r in heads:
        reduce.stage(2, r, plan.early_pick)
    for r in tails:
        reduce.stage(1, r, plan.early_pick)
    for r in heads:
        reduce.stage(3, r, plan.early_pick)
    for s in (2, 3):
        for r in tails:
            reduce.stage(s, r, plan.early_pick)
    reduce.finish(own)
    reduce.drain()
    for b in range(NB):
        rows = pl.ds(b * BLK, BLK)
        pltpu.make_async_copy(xs.at[rows], out_hbm.at[rows], outs.at[b]).wait()
        pltpu.make_async_copy(resid0.at[rows], gin_hbm.at[rows], gins.at[b]).wait()


def layer(plan, lens, ids, feat, x, cot, chunk):
    S = jax.ShapeDtypeStruct
    V = pltpu.VMEM
    DM = pltpu.SemaphoreType.DMA
    nz, n = plan.nz, plan.rows
    vm = pl.BlockSpec(memory_space=pltpu.VMEM)
    hb = pl.BlockSpec(memory_space=pl.ANY)

    def kernel(*refs):
        body(plan, *refs)

    return pl.pallas_call(
        kernel,
        out_shape=[S((T, D), BF), S((T, D), F32), S((n, ROW), F32)],
        in_specs=[pl.BlockSpec(memory_space=pltpu.SMEM), vm, vm, hb, hb, hb],
        out_specs=[hb, hb, vm],
        scratch_shapes=[
            V((nz, 2, 2, 2, n, ROW), BF), V((plan.padded, ROW), BF), V((4, 2048, 128), F32),
            V((3, D, D), BF), V((4, D, D), BF), V((D, D), BF), V((2048, D), BF), V((256 + TAIL, D), BF),
            V((T, D), BF), V((T, D), BF), V((T, D), F32), V((T, D), BF), V((12, T, 128), BF),
            V((PAIRS, T, 128), BF), V((8, T), F32), V((8, D), F32),
            V((4, T, D), BF), V((4, T, D), BF), V((T, D), BF), V((T, D), BF), V((T, D), BF), V((T, D), F32),
            V((PAIRS, T, 128), BF), V((12, T, 128), BF), V((2, T, 128), F32), V((16, D), F32), V((8, D), F32),
            V((TAIL, D), F32),
            DM((nz, 2, 2)), DM((nz, 2)), DM((nz, AG_KINDS)), DM((nz, AG_KINDS)),
            DM((nz, 2, 2)), DM((nz, 2, 2)), DM((nz, RS_KINDS)), DM((nz, RS_KINDS)), DM((nz,)), DM((nz,)),
            pltpu.SemaphoreType.REGULAR, DM((3,)), DM((NB,)), DM((NB,)),
        ],
        compiler_params=pltpu.CompilerParams(
            collective_id=0, has_side_effects=True, vmem_limit_bytes=67043328
        ),
        name="layer",
    )(lens, ids, feat, x, cot, chunk)


def time_features(steps):
    half = 128
    freqs = jnp.exp(-math.log(10000.0) * jnp.arange(half, dtype=F32) / half)
    ang = steps.astype(F32).reshape(4, 1) * freqs
    f = jnp.concatenate([jnp.sin(ang), jnp.cos(ang)], axis=-1).astype(BF)
    return jnp.pad(f, ((0, 4), (0, 0)))


def shards(inputs, noisy_ids, timesteps, doc_lens, cotangent, params, momentum, average):
    ndp, nfs = lax.axis_size("dp"), lax.axis_size("fsdp")
    device_count = ndp * nfs
    row_count, seq_len, model_width = inputs.shape
    plan = Plan(ndp, nfs, params.shape[0] * device_count)
    i = lax.axis_index("dp") * nfs + lax.axis_index("fsdp")
    offset = lax.rem(i * plan.share, ROW * TILE)
    chunk = lax.dynamic_update_slice(
        jnp.zeros((plan.rows * ROW,), BF), params.astype(BF), (offset,)
    ).reshape(plan.rows, ROW)
    output, input_grad, owned = layer(
        plan, doc_lens, noisy_ids, time_features(timesteps),
        inputs.reshape(T, D), cotangent.reshape(T, D), chunk,
    )
    owned_grad = lax.dynamic_slice(owned.reshape(-1), (offset,), (plan.share,))
    gradient = owned_grad * (1.0 / math.sqrt(row_count * seq_len * device_count))
    new_momentum = MOMENTUM_RATE * momentum + gradient
    new_params = params - LEARN_RATE * (gradient + MOMENTUM_RATE * new_momentum)
    new_average = AVERAGE_RATE * average + (1.0 - AVERAGE_RATE) * new_params
    return (
        output.reshape(row_count, seq_len, model_width),
        input_grad.reshape(row_count, seq_len, model_width),
        new_params,
        new_momentum,
        new_average,
        new_params.astype(BF),
    )


def solution(mesh):
    rows = ("dp", "fsdp")
    in_specs = (
        P(rows, None, None), P(rows, None), P(rows, None), P(rows, None), P(rows, None, None),
        P(rows), P(rows), P(rows),
    )
    out_specs = (P(rows, None, None), P(rows, None, None), P(rows), P(rows), P(rows), P(rows))
    return jax.shard_map(shards, mesh=mesh, in_specs=in_specs, out_specs=out_specs, check_vma=False)
```

time: 242 us -> 176 us (0.73); the launches traced: 242 us -> 173 us
  Pallas kernels: 227 us -> 160 us
  other arithmetic: 10.4 us -> 5.37 us
  local copies, waits for them, and re-layouts: 4.07 us -> 6.77 us
    pallas_call x5 -> x1, Pallas kernels: 227 us -> 160 us  [layer(): pl.pallas_call(kernel, out_shape=[S((T, D), BF), S((T, D), F32), S((n, RO...]
    concatenate x1 -> x0, other arithmetic: 6.04 us -> none  [shards(): rows = jnp.concatenate([ga, gmid, gt], axis=0)]
    unnamed x9 -> x11, local copies, waits for them, and re-layouts: 1.15 us -> 3.86 us
where the time goes in v1:
time: 176 us; the launch traced here: 173 us
  Pallas kernels  160 us (91%)
  local copies, waits for them, and re-layouts  6.77 us (4%)
  other arithmetic  5.37 us (3%)
    pallas_call x1, Pallas kernels, layer(): pl.pallas_call(kernel, out_shape=[S((T, D), BF), S((T, D), F32), S((n, RO...  160 us
    unnamed x11, local copies, waits for them, and re-layouts  3.86 us

profile of v1, /device:TPU:0, one launch (start us, length us, event | category | flops | bytes accessed | tf_op | source)
XLA Modules:
  0.0 172.8 jit_solution(12579407832966383515)
XLA Ops:
  0.6 0.7 convert_bitcast_fusion
  1.3 0.1 fusion.3
  1.4 0.6 fusion.2.refs_2_
  2.0 1.0 convert_element_type.13
  3.1 2.1 %dynamic_update_slice.3 = bf16[114688]{0:T(1024)(128)(2,1)S(1)} dynamic-update-slice(bf16[114688]{0:T(1024)(128)(2,1)S(1)} %broadcast_in_dim.4, bf16[103024]{0:T(1024)(128)(2,1)S(1)} %convert_element_type.13, s32[]{:T(128)S(6)} %select_n.4) | dynamic-update-slice | bytes 412100 | tf_op jit(solution)/shard_map/dynamic_update_slice | solution.py:767
  5.2 0.8 reshape.39.refs_5_
  6.0 160.0 %layer.1 = (bf16[1024,512]{1,0:T(8,128)(2,1)}, f32[1024,512]{1,0:T(8,128)}, f32[224,512]{1,0:T(8,128)}) custom-call(s32[1,4]{1,0:T(1,128)} %refs_0_.1, s32[1,1024]{1,0:T(1,128)} %refs_1_.1, bf16[8,256]{1,0:T(8,128)(2,1)} %fusion.2.refs_2_, bf16[1024,512]{1,0:T(8,128)(2,1)} %bitcast.10, bf16[1024,512]{1,0:T(8,128)(2,1)} %bitcast.11, ...), custom_call_target="tpu_custom_call" | custom-call | tf_op jit(solution)/shard_map/layer/pallas_call | solution.py:728
  166.0 0.0 copy-start.3
  166.0 0.0 copy-start.2
  166.0 1.2 copy.14
  167.2 2.1 %fusion.5 = (bf16[103024]{0:T(1024)(128)(2,1)}, f32[103024]{0:T(1024)S(1)}, f32[103024]{0:T(1024)}) fusion(f32[103024]{0:T(1024)} %param.13, f32[114688]{0:T(1024)S(1)} %bitcast.9, s32[]{:T(128)S(6)} %select_n.4, f32[103024]{0:T(1024)} %param.14), kind=kLoop, calls=%fused_computation.14 | loop fusion | flops 824192 | bytes 2266532 | tf_op jit(solution)/shard_map/convert_element_type | solution.py:785
  169.4 0.0 copy-start.1
  169.4 0.0 copy-start
  169.4 0.0 copy-done.3
  169.4 0.8 multiply_add_fusion
  170.2 0.0 copy-done.2
  170.2 1.0 copy.18
  171.2 0.3 copy-done
  171.5 1.3 copy.19
  172.8 0.0 copy-done.1
  (2 shorter events, 0.0 us)
Async XLA Ops:
  166.0 3.4 %copy-start.3 = (f32[103024]{0:T(1024)S(1)}, f32[103024]{0:T(1024)}, u32[]{:S(2)}) copy-start(f32[103024]{0:T(1024)} %param.15) | copy-start | bytes 1236292
  166.0 4.2 %copy-start.2 = (bf16[1024,512]{1,0:T(8,128)(2,1)S(1)}, bf16[1024,512]{1,0:T(8,128)(2,1)}, u32[]{:S(2)}) copy-start(bf16[1024,512]{1,0:T(8,128)(2,1)} %get-tuple-element.9) | copy-start | bytes 3145732
  169.4 3.4 %copy-start.1 = (f32[103024]{0:T(1024)}, f32[103024]{0:T(1024)S(1)}, u32[]{:S(2)}) copy-start(f32[103024]{0:T(1024)S(1)} %get-tuple-element.25) | copy-start | bytes 1236292
  169.4 2.1 %copy-start = (f32[1024,512]{1,0:T(8,128)S(1)}, f32[1024,512]{1,0:T(8,128)}, u32[]{:S(2)}) copy-start(f32[1024,512]{1,0:T(8,128)} %get-tuple-element.10) | copy-start | bytes 6291460

commit v2 on v1

--- a/solution.py
+++ b/solution.py
@@ -49,6 +49,16 @@
         self.hi = last if self.only else first // layer - 1
         self.early = list(range(self.lo)) + list(range(last if self.only else self.hi + 1, self.nz))
         self.late = list(range(self.lo, self.hi + 1))
+        self.ends = [r for r in self.early if r >= self.lo]
+        self.owners = [i for i in range(self.count) if self.starts[i] + self.rows > ROW_T]
+        self.slices = PAIRS if self.lo == 1 else 1
+        self.units = [(r, None) for r in range(self.lo, self.nz)]
+        self.body_units = len(self.units)
+        for j in range(self.slices):
+            self.units += [(r, None if self.slices == 1 else j) for r in range(self.lo)]
+
+    def slice_units(self, j):
+        return range(self.body_units + j * self.lo, self.body_units + (j + 1) * self.lo)
 
     def early_pick(self, r, cx, cy):
         if self.only and r == self.nz - 1:
@@ -79,6 +89,9 @@
         y = self.y if y is None else y
         c = self.c if c is None else c
         return (z * 2 + x, y * 2 + c)
+
+    def here(self):
+        return ((self.z * 2 + self.x) * 2 + self.y) * 2 + self.c
 
     def partners(self):
         nz = self.plan.nz
@@ -204,129 +217,174 @@
         self.p, self.src, self.g = p, src, g
         self.cs, self.cr, self.ps, self.pr, self.zs, self.zr = cs, cr, ps, pr, zs, zr
         self.h, self.n = p.plan.half, p.plan.rows
-        self.a, self.b = pl.ds(0, self.h), pl.ds(self.h, self.n - self.h)
+        self.a, self.b, self.w = pl.ds(0, self.h), pl.ds(self.h, self.n - self.h), pl.ds(0, self.n)
+
+    def cols(self, j):
+        return pl.ds(0, ROW) if j is None else pl.ds(128 * j, 128)
 
     def rows(self, r, xx, yy, cc):
         plan = self.p.plan
         i = ((r * 2 + xx) * 2 + yy) * 2 + cc
         return pl.ds(pl.multiple_of(lax.div(i * plan.share, jnp.int32(ROW * TILE)) * TILE, TILE), self.n)
 
-    def cb(self, r, xx, yy, *rest):
-        return self.g.at[(r, xx, yy, 0) + rest]
-
-    def pa(self, r, xx):
-        return self.g.at[r, 0, xx, 1, self.a]
-
-    def pb(self, r, yy):
-        return self.g.at[r, 0, yy, 1, self.b]
-
-    def p2(self, r, *rest):
-        return self.g.at[(r, 1, 0, 1) + rest]
-
-    def zb(self, s):
-        return self.g.at[s, 1, 1, 1]
-
-    def ccopy(self, r, xx, yy):
-        p = self.p
+    def cb(self, u, xx, yy, part):
+        r, j = self.p.plan.units[u]
+        return self.g.at[r, xx, yy, 0, part, self.cols(j)]
+
+    def pa(self, u, xx):
+        r, j = self.p.plan.units[u]
+        return self.g.at[r, 0, xx, 1, self.a, self.cols(j)]
+
+    def pb(self, u, yy):
+        r, j = self.p.plan.units[u]
+        return self.g.at[r, 0, yy, 1, self.b, self.cols(j)]
+
+    def p2(self, u, part):
+        r, j = self.p.plan.units[u]
+        return self.g.at[r, 1, 0, 1, part, self.cols(j)]
+
+    def ccopy(self, u, xx, yy):
+        p = self.p
+        r, j = p.plan.units[u]
         return rcopy(
-            self.src.at[self.rows(r, xx, yy, 1 - p.c)], self.cb(r, xx, yy),
-            self.cs.at[r, xx, yy], self.cr.at[r, xx, yy], p.C,
+            self.src.at[self.rows(r, xx, yy, 1 - p.c), self.cols(j)], self.cb(u, xx, yy, self.w),
+            self.cs.at[u, xx, yy], self.cr.at[u, xx, yy], p.C,
         )
 
-    def cp(self, r, k):
+    def cp(self, u, k):
         p = self.p
         x, y = p.x, p.y
         s, d, dev = (
-            (self.cb(r, 0, 1 - y, self.a), self.pa(r, 0), p.Y),
-            (self.cb(r, 1, 1 - y, self.a), self.pa(r, 1), p.Y),
-            (self.cb(r, 1 - x, 0, self.b), self.pb(r, 0), p.X),
-            (self.cb(r, 1 - x, 1, self.b), self.pb(r, 1), p.X),
-            (self.pa(r, 1 - x), self.p2(r, self.a), p.X),
-            (self.pb(r, 1 - y), self.p2(r, self.b), p.Y),
+            (self.cb(u, 0, 1 - y, self.a), self.pa(u, 0), p.Y),
+            (self.cb(u, 1, 1 - y, self.a), self.pa(u, 1), p.Y),
+            (self.cb(u, 1 - x, 0, self.b), self.pb(u, 0), p.X),
+            (self.cb(u, 1 - x, 1, self.b), self.pb(u, 1), p.X),
+            (self.pa(u, 1 - x), self.p2(u, self.a), p.X),
+            (self.pb(u, 1 - y), self.p2(u, self.b), p.Y),
         )[k]
-        return rcopy(s, d, self.ps.at[r, k], self.pr.at[r, k], dev)
-
-    def zcopy(self, r):
-        p = self.p
-        return rcopy(self.p2(r), self.zb(p.z), self.zs.at[r], self.zr.at[p.z], p.dev(z=r))
-
-    def zwait(self, s):
-        rcopy(self.p2(0), self.zb(s), self.zs.at[0], self.zr.at[s], self.p.dev(z=s)).wait_recv()
-
-    def stage(self, s, r, pick):
+        return rcopy(s, d, self.ps.at[u, k], self.pr.at[u, k], dev)
+
+    def zcopy(self, u):
+        p = self.p
+        r, j = p.plan.units[u]
+        k = j or 0
+        return rcopy(
+            self.p2(u, self.w), self.g.at[p.z, 1, 1, 1, self.w, self.cols(j)],
+            self.zs.at[u], self.zr.at[k, p.z], p.dev(z=r),
+        )
+
+    def zwait(self, j, s):
+        ref = self.g.at[s, 1, 1, 1, self.w, self.cols(j)]
+        rcopy(ref, ref, self.zs.at[0], self.zr.at[j or 0, s], self.p.dev(z=s)).wait_recv()
+
+    def stage(self, s, u):
         p = self.p
         z, x, y = p.z, p.x, p.y
+        r, j = p.plan.units[u]
         both = [(xx, yy) for xx in (0, 1) for yy in (0, 1)]
         if s == 0:
             for xx, yy in both:
-                when(pick(r, xx, yy))(lambda: self.ccopy(r, xx, yy).start())
+                self.ccopy(u, xx, yy).start()
         if s == 1:
             for xx, yy in both:
-                def go():
-                    self.ccopy(r, xx, yy).wait_recv()
-                    ref = self.cb(r, xx, yy)
-                    ref[...] = ref[...] + self.src[self.rows(r, xx, yy, p.c), :]
-
-                when(pick(r, xx, yy))(go)
+                self.ccopy(u, xx, yy).wait_recv()
+                ref = self.cb(u, xx, yy, self.w)
+                ref[...] = ref[...] + self.src[self.rows(r, xx, yy, p.c), self.cols(j)]
             for q in (0, 1):
-                when(pick(r, q, 1 - y))(lambda: self.cp(r, q).start())
-                when(pick(r, 1 - x, q))(lambda: self.cp(r, 2 + q).start())
+                self.cp(u, q).start()
+                self.cp(u, 2 + q).start()
         if s == 2:
             for q in (0, 1):
-                def goa():
-                    self.cp(r, q).wait_recv()
-                    ref = self.pa(r, q)
-                    ref[...] = ref[...] + self.cb(r, q, y, self.a)[...]
-
-                when(pick(r, q, y))(goa)
-            when(pick(r, 1 - x, y))(lambda: self.cp(r, 4).start())
+                self.cp(u, q).wait_recv()
+                ref = self.pa(u, q)
+                ref[...] = ref[...] + self.cb(u, q, y, self.a)[...]
+            self.cp(u, 4).start()
             for q in (0, 1):
-                def gob():
-                    self.cp(r, 2 + q).wait_recv()
-                    ref = self.pb(r, q)
-                    ref[...] = ref[...] + self.cb(r, x, q, self.b)[...]
-
-                when(pick(r, x, q))(gob)
-            when(pick(r, x, 1 - y))(lambda: self.cp(r, 5).start())
+                self.cp(u, 2 + q).wait_recv()
+                ref = self.pb(u, q)
+                ref[...] = ref[...] + self.cb(u, x, q, self.b)[...]
+            self.cp(u, 5).start()
         if s == 3:
-            def fin():
-                self.cp(r, 4).wait_recv()
-                ref = self.p2(r, self.a)
-                ref[...] = ref[...] + self.pa(r, x)[...]
-                self.cp(r, 5).wait_recv()
-                ref = self.p2(r, self.b)
-                ref[...] = ref[...] + self.pb(r, y)[...]
-
-            when(pick(r, x, y))(fin)
-            when(pick(r, x, y), z != r)(lambda: self.zcopy(r).start())
+            self.cp(u, 4).wait_recv()
+            ref = self.p2(u, self.a)
+            ref[...] = ref[...] + self.pa(u, x)[...]
+            self.cp(u, 5).wait_recv()
+            ref = self.p2(u, self.b)
+            ref[...] = ref[...] + self.pb(u, y)[...]
+            when(z != r)(lambda: self.zcopy(u).start())
 
     def finish(self, out):
-        z = self.p.z
-        out[...] = self.p2(z)[...].astype(F32)
-        for s in range(self.p.plan.nz):
+        z, plan = self.p.z, self.p.plan
+        out[...] = self.g[z, 1, 0, 1].astype(F32)
+        for s in range(plan.nz):
             def go():
-                self.zwait(s)
-                out[...] += self.zb(s)[...].astype(F32)
+                @pl.when(z >= plan.lo)
+                def _():
+                    self.zwait(None, s)
+
+                @pl.when(z < plan.lo)
+                def _():
+                    for j in range(plan.slices):
+                        self.zwait(None if plan.slices == 1 else j, s)
+
+                out[...] += self.g[s, 1, 1, 1].astype(F32)
 
             when(z != s)(go)
 
     def drain(self):
-        for r in range(self.p.plan.nz):
+        for u, (r, _) in enumerate(self.p.plan.units):
             for xx in (0, 1):
                 for yy in (0, 1):
-                    self.ccopy(r, xx, yy).wait_send()
+                    self.ccopy(u, xx, yy).wait_send()
             for k in range(RS_KINDS):
-                self.cp(r, k).wait_send()
-            when(self.p.z != r)(lambda: self.zcopy(r).wait_send())
-
-
-def pipelined(stages, layers):
-    order = []
-    for t in range(len(layers) + len(stages) - 1):
-        for s in reversed(range(len(stages))):
-            if 0 <= t - s < len(layers):
-                order.append((stages[s], layers[t - s]))
-    return order
+                self.cp(u, k).wait_send()
+            when(self.p.z != r)(lambda: self.zcopy(u).wait_send())
+
+
+class Corner:
+    def __init__(self, p, t, rx, zt, ss, rs, zs, zr):
+        self.p, self.t, self.rx, self.zt = p, t, rx, zt
+        self.ss, self.rs, self.zs, self.zr = ss, rs, zs, zr
+
+    def copy(self, k):
+        p = self.p
+        return rcopy(self.t.at[k], self.rx.at[k], self.ss.at[k], self.rs.at[k], (p.C, p.Y, p.X)[k])
+
+    def zcopy(self, m):
+        p = self.p
+        return rcopy(
+            self.t.at[3], self.zt.at[p.z], self.zs.at[m], self.zr.at[p.z], p.dev(z=p.plan.ends[m])
+        )
+
+    def senders(self, m):
+        p = self.p
+        return when(p.z != p.plan.ends[m], p.plan.early_pick(p.plan.ends[m], p.x, p.y))
+
+    def start(self):
+        self.copy(0).start()
+
+    def step(self, k):
+        self.copy(k).wait_recv()
+        self.t[k + 1] = self.t[k] + self.rx[k]
+        if k < 2:
+            self.copy(k + 1).start()
+        else:
+            for m in range(len(self.p.plan.ends)):
+                self.senders(m)(lambda: self.zcopy(m).start())
+
+    def finish(self, r):
+        p = self.p
+        self.zt[r] = self.t[3]
+        for s in range(p.plan.nz):
+            if s != r:
+                ref = self.zt.at[s]
+                rcopy(ref, ref, self.zs.at[0], self.zr.at[s], p.dev(z=s)).wait_recv()
+
+    def drain(self):
+        for k in range(3):
+            self.copy(k).wait_send()
+        for m in range(len(self.p.plan.ends)):
+            self.senders(m)(lambda: self.zcopy(m).wait_send())
 
 
 def assemble(plan, g, lo, hi, store):
@@ -431,9 +489,14 @@
 def body(plan, lens, ids, feat, x_hbm, cot_hbm, chunk_hbm, out_hbm, gin_hbm, own,
          g, src, wf, wq, wu, wo, wd, vec, xs, cs, resid0, attn_in, qkv, attended, lse, ft,
          act, dpre, fin, dff, dbr, dres, datt, dqkv, accv, slots, small, cacc,
-         zs, zr, ps, pr, rcs, rcr, rps, rpr, rzs, rzr, ready, ins, outs, gins):
+         ct, crx, czt, ht, hrx, hzt, tg,
+         zs, zr, ps, pr, rcs, rcr, rps, rpr, rzs, rzr,
+         css, crs, czs, czr, hss, hrs, hzs, hzr, ready, ins, outs, gins):
     p = Place(plan)
     nz = plan.nz
+    corner = Corner(p, ct, crx, czt, css, crs, czs, czr)
+    hints = Corner(p, ht, hrx, hzt, hss, hrs, hzs, hzr)
+    place = lax.div(lax.broadcasted_iota(jnp.int32, (32, 1), 0), jnp.int32(4)) == (p.x * 2 + p.y) * 2 + p.c
     gather = Gather(p, g, zs, zr, ps, pr)
     loads = [
         pltpu.make_async_copy(chunk_hbm, g.at[p.z, p.x, p.y, p.c], ins.at[0]),
@@ -456,6 +519,8 @@
                     when(p.far(r) == t - (s - 1))(lambda: gather.stage(s, r, plan.early_pick))
     for r in plan.late:
         gather.stage(0, r, plan.late_pick)
+    ht[0] = jnp.where(place, jnp.concatenate([feat[...].astype(F32)] * 4, axis=0), 0.0).astype(BF)
+    hints.start()
 
     def gather_hook(i):
         for s in (1, 2, 3, 4):
@@ -537,6 +602,7 @@
     assemble(plan, g, ROW_UP, ROW_DOWN, spread(wf, ROW_UP))
     assemble(plan, g, ROW_DOWN, ROW_T, wd_store)
     regroup(wf, 4, wu)
+    hints.step(0)
     gather.drain()
     signal_all(p, ready)
     small[...] = jnp.zeros_like(small)
@@ -582,6 +648,8 @@
         return 0
 
     lax.fori_loop(0, NB, feed, 0)
+    hints.step(1)
+    src[ROW_T:plan.padded, :] = jnp.zeros((plan.padded - ROW_T, ROW), BF)
     for c in range(4):
         src[ROW_DOWN + 512 * c:ROW_DOWN + 512 * c + 512, :] = mm_tn(act[c], dff[...]).astype(BF)
         put(wf, c, 4, mm_tn(fin[...], dpre[c]))
@@ -590,14 +658,45 @@
         src[ROW_O + 128 * j:ROW_O + 128 * j + 128, :] = mm_tn(attended[j], dbr[...]).astype(BF)
 
     reduce = Reduce(p, src, g, rcs, rcr, rps, rpr, rzs, rzr)
+    hints.step(2)
     wait_all(p, ready)
-    for r in plan.late:
-        reduce.stage(0, r, plan.late_pick)
+    for u in range(plan.body_units):
+        reduce.stage(0, u)
+
+    def qkv_grad(j):
+        dq = jnp.concatenate([dqkv[4 * c + j] for c in range(3)], axis=1)
+        gq = mm_tn(attn_in[...], dq)
+        for c in range(3):
+            wf[j, pl.ds(c, 512, stride=3), :] = gq[:, lanes(c)]
+        src[0:ROW_O, lanes(j)] = wf[j, 0:ROW_O, :].astype(BF)
+        for c in (0, 2):
+            slots[10 + c // 2:11 + c // 2, lanes(j)] = jnp.sum(dqkv[4 * c + j].astype(F32), axis=0, keepdims=True)
+
+    def slice_start(j):
+        qkv_grad(j)
+        if plan.slices > 1:
+            for u in plan.slice_units(j):
+                reduce.stage(0, u)
+
+    def reduce_at(s, u):
+        return lambda: reduce.stage(s, u)
+
+    steps = []
+    for k in range(plan.body_units):
+        for s, at in ((1, 1 + 3 * k), (2, 4 + 3 * k), (3, 6 + 3 * k)):
+            steps.append((at, -s, reduce_at(s, k)))
+    for j in range(PAIRS - 1):
+        steps.append((NB * (j + 1), 0, lambda j=j: slice_start(j)))
+        if plan.slices > 1:
+            for s, at in ((1, (10, 11, 14)[j]), (2, (12, 13, 15)[j]), (3, (14, 15, 16)[j])):
+                for u in plan.slice_units(j):
+                    steps.append((at, -s, reduce_at(s, u)))
+    steps.sort(key=lambda e: e[:2])
 
     def reduce_hook(i):
-        for k, r in enumerate(plan.late):
-            for s, at in ((1, 1 + 3 * k), (2, 4 + 3 * k), (3, 6 + 3 * k)):
-                when(i == min(at, PAIRS * NB))(lambda: reduce.stage(s, r, plan.late_pick))
+        for at, _, run in steps:
+            if at < PAIRS * NB:
+                pl.when(i == at)(run)
 
     def attend_back(i, _):
         reduce_hook(i)
@@ -634,20 +733,15 @@
         return 0
 
     lax.fori_loop(0, PAIRS * NB, attend_back, 0)
-    reduce_hook(PAIRS * NB)
-
-    cols = []
-    for c in range(3):
-        dq = jnp.concatenate([dqkv[4 * c + j] for j in range(4)], axis=1)
-        put(wf, c, 3, mm_tn(attn_in[...], dq))
-        if c != 1:
-            cols.append(jnp.sum(dq.astype(F32), axis=0, keepdims=True))
-    take(wf, 3, src, 0)
-    heads = [r for r in plan.early if r < plan.lo]
-    tails = [r for r in plan.early if r >= plan.lo]
-    for r in heads:
-        reduce.stage(0, r, plan.early_pick)
-    slots[...] = jnp.zeros_like(slots)
+    slice_start(PAIRS - 1)
+    last = plan.slice_units(plan.slices - 1)
+    if plan.slices == 1:
+        for u in last:
+            reduce.stage(0, u)
+    for at, _, run in steps:
+        if at >= PAIRS * NB:
+            run()
+    slots[0:10, :] = jnp.zeros((10, D), F32)
     cacc[...] = jnp.zeros_like(cacc)
 
     def embed_back(b, _):
@@ -655,8 +749,13 @@
 
         @pl.when(b == 1)
         def _():
-            for r in heads:
-                reduce.stage(1, r, plan.early_pick)
+            for u in last:
+                reduce.stage(1, u)
+
+        @pl.when(b == 3)
+        def _():
+            for u in last:
+                reduce.stage(2, u)
 
         e1 = jnp.zeros((BLK, D), F32)
         for c in range(3):
@@ -671,42 +770,54 @@
         ds = gi.astype(BF)
         oh = (lax.broadcasted_iota(jnp.int32, (32, BLK), 0) == ids[0:1, rows]).astype(F32).astype(BF)
         cacc[0:32, :] += mm(oh, ds)
-        slots[pl.ds(b, 1), :] = jnp.sum(ds.astype(F32), axis=0, keepdims=True)
+        total = jnp.sum(ds.astype(F32), axis=0, keepdims=True)
+        slots[pl.ds(b, 1), :] = total
+        slots[pl.ds(b + NB, 1), :] = total
         return 0
 
     lax.fori_loop(0, NB, embed_back, 0)
     per = slots[0:8, :]
-    total = jnp.sum(per, axis=0, keepdims=True)
-    first = lax.broadcasted_iota(jnp.int32, (8, 1), 0) == 0
+    total = 0.5 * jnp.sum(per, axis=0, keepdims=True)
+    first = lax.rem(lax.broadcasted_iota(jnp.int32, (8, 1), 0), jnp.int32(NB)) == 0
     per = jnp.where(long, jnp.where(first, total, 0.0), per)
-    src[ROW_T:ROW_C, :] = lax.dot_general(
-        feat[...].astype(F32), per, (((0,), (0,)), ((), ())),
-        precision=lax.Precision.HIGHEST, preferred_element_type=F32,
-    ).astype(BF)
+    ct[0, 0:32, :] = jnp.where(place, jnp.concatenate([per] * 4, axis=0), 0.0).astype(BF)
     o = ROW_V - ROW_C
     cacc[o:o + 2, :] = slots[8:10, :]
     cacc[o + 2:o + 4, :] = small[1:3, :]
-    cacc[o + 4:o + 5, :] = cols[0]
-    cacc[o + 5:o + 6, :] = cols[1]
+    cacc[o + 4:o + 5, :] = slots[10:11, :]
+    cacc[o + 5:o + 6, :] = slots[11:12, :]
     cacc[o + 6:o + 7, :] = small[3:4, :]
     cacc[o + 7:o + 8, :] = small[0:1, :]
     cacc[o + 8:o + 12, :] = small[4:8, :]
-    src[ROW_C:ROW_C + TAIL, :] = cacc[...].astype(BF)
-    if plan.padded > ROW_C + TAIL:
-        src[ROW_C + TAIL:plan.padded, :] = jnp.zeros((plan.padded - ROW_C - TAIL, ROW), BF)
-
-    for r in tails:
-        reduce.stage(0, r, plan.early_pick)
-    for r in heads:
-        reduce.stage(2, r, plan.early_pick)
-    for r in tails:
-        reduce.stage(1, r, plan.early_pick)
-    for r in heads:
-        reduce.stage(3, r, plan.early_pick)
-    for s in (2, 3):
-        for r in tails:
-            reduce.stage(s, r, plan.early_pick)
+    ct[0, 32:32 + TAIL, :] = cacc[...].astype(BF)
+    corner.start()
+    for u in last:
+        reduce.stage(3, u)
+    for k in range(3):
+        corner.step(k)
     reduce.finish(own)
+    for r in plan.ends:
+        def tail():
+            hints.finish(r)
+            corner.finish(r)
+            tg[0:256, :] = mm_tn(
+                jnp.concatenate([hzt[s] for s in range(nz)], axis=0),
+                jnp.concatenate([czt[s, 0:32, :] for s in range(nz)], axis=0),
+            )
+            rest = czt[0, 32:32 + TAIL, :].astype(F32)
+            for s in range(1, nz):
+                rest = rest + czt[s, 32:32 + TAIL, :].astype(F32)
+            tg[256:256 + TAIL, :] = rest
+
+        when(p.z == r, plan.early_pick(r, p.x, p.y))(tail)
+    for i in plan.owners:
+        @pl.when(p.here() == i)
+        def _():
+            at = plan.starts[i]
+            a, b = max(at, ROW_T), min(at + plan.rows, ROW_C + TAIL)
+            own[a - at:b - at, :] += tg[a - ROW_T:b - ROW_T, :]
+    hints.drain()
+    corner.drain()
     reduce.drain()
     for b in range(NB):
         rows = pl.ds(b * BLK, BLK)
@@ -718,7 +829,7 @@
     S = jax.ShapeDtypeStruct
     V = pltpu.VMEM
     DM = pltpu.SemaphoreType.DMA
-    nz, n = plan.nz, plan.rows
+    nz, n, nu, ne = plan.nz, plan.rows, len(plan.units), len(plan.ends)
     vm = pl.BlockSpec(memory_space=pltpu.VMEM)
     hb = pl.BlockSpec(memory_space=pl.ANY)
 
@@ -738,8 +849,11 @@
             V((4, T, D), BF), V((4, T, D), BF), V((T, D), BF), V((T, D), BF), V((T, D), BF), V((T, D), F32),
             V((PAIRS, T, 128), BF), V((12, T, 128), BF), V((2, T, 128), F32), V((16, D), F32), V((8, D), F32),
             V((TAIL, D), F32),
+            V((4, 32 + TAIL, D), BF), V((3, 32 + TAIL, D), BF), V((nz, 32 + TAIL, D), BF),
+            V((4, 32, 256), BF), V((3, 32, 256), BF), V((nz, 32, 256), BF), V((256 + TAIL, D), F32),
             DM((nz, 2, 2)), DM((nz, 2)), DM((nz, AG_KINDS)), DM((nz, AG_KINDS)),
-            DM((nz, 2, 2)), DM((nz, 2, 2)), DM((nz, RS_KINDS)), DM((nz, RS_KINDS)), DM((nz,)), DM((nz,)),
+            DM((nu, 2, 2)), DM((nu, 2, 2)), DM((nu, RS_KINDS)), DM((nu, RS_KINDS)), DM((nu,)), DM((PAIRS, nz)),
+            DM((3,)), DM((3,)), DM((ne,)), DM((nz,)), DM((3,)), DM((3,)), DM((ne,)), DM((nz,)),
             pltpu.SemaphoreType.REGULAR, DM((3,)), DM((NB,)), DM((NB,)),
         ],
         compiler_params=pltpu.CompilerParams(
@@ -754,7 +868,7 @@
     freqs = jnp.exp(-math.log(10000.0) * jnp.arange(half, dtype=F32) / half)
     ang = steps.astype(F32).reshape(4, 1) * freqs
     f = jnp.concatenate([jnp.sin(ang), jnp.cos(ang)], axis=-1).astype(BF)
-    return jnp.pad(f, ((0, 4), (0, 0)))
+    return jnp.concatenate([f, f], axis=0)
 
 
 def shards(inputs, noisy_ids, timesteps, doc_lens, cotangent, params, momentum, average):

time: 176 us -> 167 us (0.949)
  Pallas kernels: 160 us -> 151 us
    pallas_call x1, Pallas kernels: 160 us -> 151 us  [layer(): pl.pallas_call(kernel, out_shape=[S((T, D), BF), S((T, D), F32), S((n, RO...]
where the time goes in v2:
time: 167 us; the launch traced here: 164 us
  Pallas kernels  151 us (90%)
  local copies, waits for them, and re-layouts  6.77 us (4%)
  other arithmetic  5.38 us (3%)
    pallas_call x1, Pallas kernels, layer(): pl.pallas_call(kernel, out_shape=[S((T, D), BF), S((T, D), F32), S((n, RO...  151 us
    unnamed x11, local copies, waits for them, and re-layouts  3.86 us

profile of v2, /device:TPU:0, one launch (start us, length us, event | category | flops | bytes accessed | tf_op | source)
XLA Modules:
  0.0 164.3 jit_solution(13697469598311875192)
XLA Ops:
  0.6 0.7 convert_bitcast_fusion
  1.3 0.1 fusion
  1.4 0.6 maximum_maximum_fusion.refs_2_
  2.0 1.0 convert_element_type.11
  3.1 2.1 %dynamic_update_slice.3 = bf16[114688]{0:T(1024)(128)(2,1)S(1)} dynamic-update-slice(bf16[114688]{0:T(1024)(128)(2,1)S(1)} %broadcast_in_dim.4, bf16[103024]{0:T(1024)(128)(2,1)S(1)} %convert_element_type.11, s32[]{:T(128)S(6)} %select_n.4) | dynamic-update-slice | bytes 412100 | tf_op jit(solution)/shard_map/dynamic_update_slice | solution.py:881
  5.2 0.8 reshape.39.refs_5_
  6.0 151.4 %layer.1 = (bf16[1024,512]{1,0:T(8,128)(2,1)}, f32[1024,512]{1,0:T(8,128)}, f32[224,512]{1,0:T(8,128)}) custom-call(s32[1,4]{1,0:T(1,128)} %refs_0_.1, s32[1,1024]{1,0:T(1,128)} %refs_1_.1, bf16[8,256]{1,0:T(8,128)(2,1)} %maximum_maximum_fusion.refs_2_, bf16[1024,512]{1,0:T(8,128)(2,1)} %bitcast.10, bf16[1024,512]{1,0:T(8,128)(2,1)} %bitcast.11, ...), custom_call_target="tpu_custom_call" | custom-call | tf_op jit(solution)/shard_map/layer/pallas_call | solution.py:839
  157.5 0.0 copy-start.3
  157.5 0.0 copy-start.2
  157.5 1.2 copy.14
  158.7 2.1 %fusion.2 = (bf16[103024]{0:T(1024)(128)(2,1)}, f32[103024]{0:T(1024)S(1)}, f32[103024]{0:T(1024)}) fusion(f32[103024]{0:T(1024)} %param.13, f32[114688]{0:T(1024)S(1)} %bitcast.9, s32[]{:T(128)S(6)} %select_n.4, f32[103024]{0:T(1024)} %param.14), kind=kLoop, calls=%fused_computation.11 | loop fusion | flops 824192 | bytes 2266532 | tf_op jit(solution)/shard_map/convert_element_type | solution.py:899
  160.9 0.0 copy-start.1
  160.9 0.0 copy-start
  160.9 0.0 copy-done.3
  160.9 0.8 multiply_add_fusion
  161.7 0.0 copy-done.2
  161.7 1.0 copy.18
  162.7 0.3 copy-done
  163.0 1.3 copy.19
  164.3 0.0 copy-done.1
  (2 shorter events, 0.0 us)
Async XLA Ops:
  157.5 3.4 %copy-start.3 = (f32[103024]{0:T(1024)S(1)}, f32[103024]{0:T(1024)}, u32[]{:S(2)}) copy-start(f32[103024]{0:T(1024)} %param.15) | copy-start | bytes 1236292
  157.5 4.2 %copy-start.2 = (bf16[1024,512]{1,0:T(8,128)(2,1)S(1)}, bf16[1024,512]{1,0:T(8,128)(2,1)}, u32[]{:S(2)}) copy-start(bf16[1024,512]{1,0:T(8,128)(2,1)} %get-tuple-element.9) | copy-start | bytes 3145732
  160.9 3.4 %copy-start.1 = (f32[103024]{0:T(1024)}, f32[103024]{0:T(1024)S(1)}, u32[]{:S(2)}) copy-start(f32[103024]{0:T(1024)S(1)} %get-tuple-element.25) | copy-start | bytes 1236292
  160.9 2.1 %copy-start = (f32[1024,512]{1,0:T(8,128)S(1)}, f32[1024,512]{1,0:T(8,128)}, u32[]{:S(2)}) copy-start(f32[1024,512]{1,0:T(8,128)} %get-tuple-element.10) | copy-start | bytes 6291460

commit v3 on v2

--- a/solution.py
+++ b/solution.py
@@ -22,6 +22,7 @@
 NB = T // BLK
 PAIRS = 4
 SCALE = 0.125
+LOG2E = math.log2(math.e)
 ROW_O, ROW_UP, ROW_DOWN, ROW_T, ROW_C, ROW_V = 1536, 2048, 4096, 6144, 6400, 6427
 TAIL = 48
 AG_KINDS = 13
@@ -51,6 +52,7 @@
         self.late = list(range(self.lo, self.hi + 1))
         self.ends = [r for r in self.early if r >= self.lo]
         self.owners = [i for i in range(self.count) if self.starts[i] + self.rows > ROW_T]
+        self.flat = -(-self.share // 1024) * 8
         self.slices = PAIRS if self.lo == 1 else 1
         self.units = [(r, None) for r in range(self.lo, self.nz)]
         self.body_units = len(self.units)
@@ -403,6 +405,35 @@
             store(a, b, g[at(i) + (slice(a - s, b - s),)])
 
 
+class Shift:
+    def __init__(self, plan, p):
+        self.p, self.n, self.flat = p, plan.rows, plan.flat
+        at = lax.rem(p.here() * plan.share, jnp.int32(ROW * TILE))
+        self.q, self.s = lax.div(at, jnp.int32(128)), lax.rem(at, jnp.int32(128))
+        self.high = lax.broadcasted_iota(jnp.int32, (1, 128), 1) >= self.s
+
+    def load(self, wf, g):
+        p, n, f = self.p, self.n, self.flat
+        wf[0, 0:72, :] = jnp.zeros((72, 128), F32)
+        wf[0, 72:72 + f, :] = pltpu.roll(wf[1, 0:f, :], self.s, 1)
+        if 4 * n > f:
+            wf[0, 72 + f:72 + 4 * n, :] = jnp.zeros((4 * n - f, 128), F32)
+        a = wf[0, pl.ds(72 - self.q, 4 * n), :]
+        b = wf[0, pl.ds(71 - self.q, 4 * n), :]
+        wf[2, 0:4 * n, :] = jnp.where(self.high, a, b)
+        for j in range(4):
+            g[p.z, p.x, p.y, p.c, :, lanes(j)] = wf[2, pl.ds(j, n, stride=4), :].astype(BF)
+
+    def store(self, wf, own, out):
+        n, f = self.n, self.flat
+        for j in range(4):
+            wf[0, pl.ds(j, n, stride=4), :] = own[:, lanes(j)]
+        wf[0, 4 * n:4 * n + 16, :] = jnp.zeros((16, 128), F32)
+        a = wf[0, pl.ds(self.q, f), :]
+        b = wf[0, pl.ds(self.q + 1, f), :]
+        out[...] = pltpu.roll(jnp.where(self.high, a, b), lax.rem(128 - self.s, jnp.int32(128)), 1)
+
+
 def mm(a, b):
     return lax.dot_general(a, b, (((1,), (0,)), ((), ())), preferred_element_type=F32)
 
@@ -486,10 +517,10 @@
     return pl.ds(pl.multiple_of(b * BLK, BLK), BLK)
 
 
-def body(plan, lens, ids, feat, x_hbm, cot_hbm, chunk_hbm, out_hbm, gin_hbm, own,
+def body(plan, lens, ids, feat, x_hbm, cot_hbm, chunk_hbm, out_hbm, gin_hbm, own_flat,
          g, src, wf, wq, wu, wo, wd, vec, xs, cs, resid0, attn_in, qkv, attended, lse, ft,
          act, dpre, fin, dff, dbr, dres, datt, dqkv, accv, slots, small, cacc,
-         ct, crx, czt, ht, hrx, hzt, tg,
+         ct, crx, czt, ht, hrx, hzt, tg, own,
          zs, zr, ps, pr, rcs, rcr, rps, rpr, rzs, rzr,
          css, crs, czs, czr, hss, hrs, hzs, hzr, ready, ins, outs, gins):
     p = Place(plan)
@@ -499,7 +530,7 @@
     place = lax.div(lax.broadcasted_iota(jnp.int32, (32, 1), 0), jnp.int32(4)) == (p.x * 2 + p.y) * 2 + p.c
     gather = Gather(p, g, zs, zr, ps, pr)
     loads = [
-        pltpu.make_async_copy(chunk_hbm, g.at[p.z, p.x, p.y, p.c], ins.at[0]),
+        pltpu.make_async_copy(chunk_hbm, wf.at[1, pl.ds(0, plan.flat)], ins.at[0]),
         pltpu.make_async_copy(x_hbm, xs, ins.at[1]),
         pltpu.make_async_copy(cot_hbm, cs, ins.at[2]),
     ]
@@ -507,8 +538,10 @@
         cpy.start()
     bar = pltpu.get_barrier_semaphore()
     signal_all(p, bar)
+    shift = Shift(plan, p)
+    loads[0].wait()
+    shift.load(wf, g)
     wait_all(p, bar)
-    loads[0].wait()
 
     for r in plan.early:
         gather.stage(0, r, plan.early_pick)
@@ -557,7 +590,7 @@
         for c in range(3):
             pr_ = mm(a, wq[c])
             if c == 0:
-                pr_ = pr_ + bq
+                pr_ = (pr_ + bq) * (SCALE * LOG2E)
             if c == 2:
                 pr_ = pr_ + bv
             pr_ = pr_.astype(BF)
@@ -572,7 +605,7 @@
         gather_hook(i + NB)
         pair, qb = lax.div(i, NB), lax.rem(i, NB)
         rows = block_rows(qb)
-        q = qkv[pair, rows, :] * jnp.asarray(SCALE, BF)
+        q = qkv[pair, rows, :]
         k = qkv[PAIRS + pair]
         va = jnp.concatenate([qkv[2 * PAIRS + pair], ones], axis=1)
         bias = key_bias(lens, qb)
@@ -581,9 +614,9 @@
             qm = jnp.where(lane_half(par), q, jnp.zeros_like(q))
             s = mm_nt(k, qm) + bias
             m = jnp.max(s, axis=0, keepdims=True)
-            e = jnp.exp(s - m)
+            e = jnp.exp2(s - m)
             l = jnp.sum(e, axis=0, keepdims=True)
-            lse[pl.ds(2 * pair + par, 1), rows] = m + jnp.log(l)
+            lse[pl.ds(2 * pair + par, 1), rows] = m + jnp.log(l) * LOG2E
             oa = mm_tn(e.astype(BF), va)
             heads.append(oa[:, :128] / oa[:, 128:])
         attended[pair, rows, :] = jnp.where(lane_half(0), heads[0], heads[1]).astype(BF)
@@ -634,7 +667,7 @@
             acc = acc + mm(a, wdc)
             e2 = e2 + mm_nt(dp, wu[c])
         xs[rows, :] = acc.astype(BF)
-        pltpu.make_async_copy(xs.at[rows], out_hbm.at[rows], outs.at[b]).start()
+        pltpu.make_async_copy(xs.at[rows], out_hbm.at[0, rows], outs.at[b]).start()
         small[1:2, :] += jnp.sum(e2 * n, axis=0, keepdims=True)
         small[2:3, :] += jnp.sum(e2, axis=0, keepdims=True)
         dr = do + norm_back(e2 * g2, n, inv)
@@ -698,15 +731,21 @@
             if at < PAIRS * NB:
                 pl.when(i == at)(run)
 
+    head = lax.broadcasted_iota(jnp.int32, (8, 128), 1) // 64
+    both = jnp.where(head == lax.broadcasted_iota(jnp.int32, (8, 128), 0), 1.0, 0.0).astype(BF)
+
     def attend_back(i, _):
         reduce_hook(i)
         pair, qb = lax.div(i, NB), lax.rem(i, NB)
         rows = block_rows(qb)
-        q = qkv[pair, rows, :] * jnp.asarray(SCALE, BF)
+        q = qkv[pair, rows, :]
         k = qkv[PAIRS + pair]
         v = qkv[2 * PAIRS + pair]
         do = datt[pair, rows, :]
         bias = key_bias(lens, qb)
+        prod = attended[pair, rows, :].astype(F32) * do.astype(F32)
+        high = prod.astype(BF)
+        delta = mm_nt(both, high) + mm_nt(both, (prod - high.astype(F32)).astype(BF))
         dqs = []
 
         @pl.when(qb == 0)
@@ -717,10 +756,9 @@
             half = lane_half(par)
             qm = jnp.where(half, q, jnp.zeros_like(q))
             dm = jnp.where(half, do, jnp.zeros_like(do))
-            pp = jnp.exp(mm_nt(k, qm) + bias - lse[pl.ds(2 * pair + par, 1), rows])
+            pp = jnp.exp2(mm_nt(k, qm) + bias - lse[pl.ds(2 * pair + par, 1), rows])
             dp = mm_nt(v, dm)
-            delta = jnp.sum(pp * dp, axis=0, keepdims=True)
-            ds = (pp * (dp - delta)).astype(BF)
+            ds = (pp * (dp - delta[par:par + 1])).astype(BF)
             accv[1] += mm(pp.astype(BF), dm)
             accv[0] += mm(ds, qm)
             dqs.append(mm_tn(ds, k))
@@ -728,7 +766,7 @@
 
         @pl.when(qb == NB - 1)
         def _():
-            dqkv[PAIRS + pair] = accv[0].astype(BF)
+            dqkv[PAIRS + pair] = (accv[0] * (1.0 / LOG2E)).astype(BF)
             dqkv[2 * PAIRS + pair] = accv[1].astype(BF)
         return 0
 
@@ -766,7 +804,7 @@
         slots[9:10, :] += jnp.sum(e1, axis=0, keepdims=True)
         gi = dres[rows, :] + norm_back(e1 * g1, n, inv)
         resid0[rows, :] = gi
-        pltpu.make_async_copy(resid0.at[rows], gin_hbm.at[rows], gins.at[b]).start()
+        pltpu.make_async_copy(resid0.at[rows], gin_hbm.at[0, rows], gins.at[b]).start()
         ds = gi.astype(BF)
         oh = (lax.broadcasted_iota(jnp.int32, (32, BLK), 0) == ids[0:1, rows]).astype(F32).astype(BF)
         cacc[0:32, :] += mm(oh, ds)
@@ -816,13 +854,14 @@
             at = plan.starts[i]
             a, b = max(at, ROW_T), min(at + plan.rows, ROW_C + TAIL)
             own[a - at:b - at, :] += tg[a - ROW_T:b - ROW_T, :]
+    shift.store(wf, own, own_flat)
     hints.drain()
     corner.drain()
     reduce.drain()
     for b in range(NB):
         rows = pl.ds(b * BLK, BLK)
-        pltpu.make_async_copy(xs.at[rows], out_hbm.at[rows], outs.at[b]).wait()
-        pltpu.make_async_copy(resid0.at[rows], gin_hbm.at[rows], gins.at[b]).wait()
+        pltpu.make_async_copy(xs.at[rows], out_hbm.at[0, rows], outs.at[b]).wait()
+        pltpu.make_async_copy(resid0.at[rows], gin_hbm.at[0, rows], gins.at[b]).wait()
 
 
 def layer(plan, lens, ids, feat, x, cot, chunk):
@@ -838,7 +877,7 @@
 
     return pl.pallas_call(
         kernel,
-        out_shape=[S((T, D), BF), S((T, D), F32), S((n, ROW), F32)],
+        out_shape=[S((1, T, D), BF), S((1, T, D), F32), S((plan.flat, 128), F32)],
         in_specs=[pl.BlockSpec(memory_space=pltpu.SMEM), vm, vm, hb, hb, hb],
         out_specs=[hb, hb, vm],
         scratch_shapes=[
@@ -850,7 +889,7 @@
             V((PAIRS, T, 128), BF), V((12, T, 128), BF), V((2, T, 128), F32), V((16, D), F32), V((8, D), F32),
             V((TAIL, D), F32),
             V((4, 32 + TAIL, D), BF), V((3, 32 + TAIL, D), BF), V((nz, 32 + TAIL, D), BF),
-            V((4, 32, 256), BF), V((3, 32, 256), BF), V((nz, 32, 256), BF), V((256 + TAIL, D), F32),
+            V((4, 32, 256), BF), V((3, 32, 256), BF), V((nz, 32, 256), BF), V((256 + TAIL, D), F32), V((n, ROW), F32),
             DM((nz, 2, 2)), DM((nz, 2)), DM((nz, AG_KINDS)), DM((nz, AG_KINDS)),
             DM((nu, 2, 2)), DM((nu, 2, 2)), DM((nu, RS_KINDS)), DM((nu, RS_KINDS)), DM((nu,)), DM((PAIRS, nz)),
             DM((3,)), DM((3,)), DM((ne,)), DM((nz,)), DM((3,)), DM((3,)), DM((ne,)), DM((nz,)),
@@ -876,23 +915,19 @@
     device_count = ndp * nfs
     row_count, seq_len, model_width = inputs.shape
     plan = Plan(ndp, nfs, params.shape[0] * device_count)
-    i = lax.axis_index("dp") * nfs + lax.axis_index("fsdp")
-    offset = lax.rem(i * plan.share, ROW * TILE)
-    chunk = lax.dynamic_update_slice(
-        jnp.zeros((plan.rows * ROW,), BF), params.astype(BF), (offset,)
-    ).reshape(plan.rows, ROW)
+    chunk = jnp.pad(params, (0, plan.flat * 128 - plan.share)).reshape(plan.flat, 128)
     output, input_grad, owned = layer(
         plan, doc_lens, noisy_ids, time_features(timesteps),
         inputs.reshape(T, D), cotangent.reshape(T, D), chunk,
     )
-    owned_grad = lax.dynamic_slice(owned.reshape(-1), (offset,), (plan.share,))
+    owned_grad = owned.reshape(-1)[:plan.share]
     gradient = owned_grad * (1.0 / math.sqrt(row_count * seq_len * device_count))
     new_momentum = MOMENTUM_RATE * momentum + gradient
     new_params = params - LEARN_RATE * (gradient + MOMENTUM_RATE * new_momentum)
     new_average = AVERAGE_RATE * average + (1.0 - AVERAGE_RATE) * new_params
     return (
-        output.reshape(row_count, seq_len, model_width),
-        input_grad.reshape(row_count, seq_len, model_width),
+        output,
+        input_grad,
         new_params,
         new_momentum,
         new_average,

time: 167 us -> 160 us (0.958)
  Pallas kernels: 151 us -> 147 us
  local copies, waits for them, and re-layouts: 6.77 us -> 4.39 us
    pallas_call x1, Pallas kernels: 151 us -> 147 us  [layer(): pl.pallas_call(kernel, out_shape=[S((1, T, D), BF), S((1, T, D), F32), S(...]
    dynamic_update_slice x1 -> x0, local copies, waits for them, and re-layouts: 2.06 us -> none  [shards(): lax.dynamic_update_slice(jnp.zeros((plan.rows * ROW,), BF), params.astype...]
    unnamed x11 -> x10, local copies, waits for them, and re-layouts: 3.86 us -> 2.61 us
where the time goes in v3:
time: 160 us; the launch traced here: 157 us
  Pallas kernels  147 us (92%)
  other arithmetic  4.51 us (3%)
  local copies, waits for them, and re-layouts  4.39 us (3%)
    pallas_call x1, Pallas kernels, layer(): pl.pallas_call(kernel, out_shape=[S((1, T, D), BF), S((1, T, D), F32), S(...  147 us

profile of v3, /device:TPU:0, one launch (start us, length us, event | category | flops | bytes accessed | tf_op | source)
XLA Modules:
  0.0 156.7 jit_solution(11502945306556350301)
XLA Ops:
  0.6 0.7 convert_bitcast_fusion
  1.3 0.1 fusion
  1.4 0.6 maximum_maximum_fusion.refs_2_
  2.0 1.8 %pad_bitcast_fusion.refs_5_ = f32[808,128]{1,0:T(8,128)} fusion(f32[103024]{0:T(1024)} %param.13), kind=kLoop, calls=%fused_computation.4 | loop fusion | bytes 825792 | tf_op jit(solution)/shard_map/reshape | solution.py:918
  3.8 147.2 %layer.1 = (bf16[1,1024,512]{2,1,0:T(8,128)(2,1)}, f32[1,1024,512]{2,1,0:T(8,128)}, f32[808,128]{1,0:T(8,128)}) custom-call(s32[1,4]{1,0:T(1,128)} %refs_0_.1, s32[1,1024]{1,0:T(1,128)} %refs_1_.1, bf16[8,256]{1,0:T(8,128)(2,1)} %maximum_maximum_fusion.refs_2_, bf16[1024,512]{1,0:T(8,128)(2,1)} %bitcast.7, bf16[1024,512]{1,0:T(8,128)(2,1)} %bitcast.8, ...), custom_call_target="tpu_custom_call" | custom-call | tf_op jit(solution)/shard_map/layer/pallas_call | solution.py:878
  151.0 0.0 copy-start.3
  151.0 0.0 copy-start.2
  151.0 2.3 %fusion.2 = (bf16[103024]{0:T(1024)(128)(2,1)}, f32[103024]{0:T(1024)S(1)}, f32[103024]{0:T(1024)}) fusion(f32[103024]{0:T(1024)} %param.13, f32[103424]{0:T(1024)} %bitcast.9, f32[103024]{0:T(1024)} %param.14), kind=kLoop, calls=%fused_computation.12 | loop fusion | flops 824192 | bytes 2266528 | tf_op jit(solution)/shard_map/convert_element_type | solution.py:934
  153.3 0.0 copy-start.1
  153.3 0.0 copy-start
  153.3 0.0 copy-done.3
  153.3 0.8 multiply_add_fusion
  154.1 0.0 copy-done.2
  154.1 1.0 copy.16
  155.1 0.3 copy-done
  155.4 1.3 copy.17
  156.7 0.0 copy-done.1
  (1 shorter events, 0.0 us)
Async XLA Ops:
  151.0 2.3 %copy-start.3 = (f32[103024]{0:T(1024)S(1)}, f32[103024]{0:T(1024)}, u32[]{:S(2)}) copy-start(f32[103024]{0:T(1024)} %param.15) | copy-start | bytes 1236292
  151.0 3.1 %copy-start.2 = (bf16[1,1024,512]{2,1,0:T(8,128)(2,1)S(1)}, bf16[1,1024,512]{2,1,0:T(8,128)(2,1)}, u32[]{:S(2)}) copy-start(bf16[1,1024,512]{2,1,0:T(8,128)(2,1)} %get-tuple-element.23) | copy-start | bytes 3145732
  153.3 3.4 %copy-start.1 = (f32[103024]{0:T(1024)}, f32[103024]{0:T(1024)S(1)}, u32[]{:S(2)}) copy-start(f32[103024]{0:T(1024)S(1)} %get-tuple-element.25) | copy-start | bytes 1236292
  153.3 2.1 %copy-start = (f32[1,1024,512]{2,1,0:T(8,128)S(1)}, f32[1,1024,512]{2,1,0:T(8,128)}, u32[]{:S(2)}) copy-start(f32[1,1024,512]{2,1,0:T(8,128)} %get-tuple-element.24) | copy-start | bytes 6291460

commit v4 on v3

--- a/solution.py
+++ b/solution.py
@@ -716,7 +716,7 @@
 
     steps = []
     for k in range(plan.body_units):
-        for s, at in ((1, 1 + 3 * k), (2, 4 + 3 * k), (3, 6 + 3 * k)):
+        for s, at in ((1, 1 + 4 * k), (2, 4 + 4 * k), (3, 7 + 4 * k)):
             steps.append((at, -s, reduce_at(s, k)))
     for j in range(PAIRS - 1):
         steps.append((NB * (j + 1), 0, lambda j=j: slice_start(j)))

time: 160 us -> 159 us (level)
  no operation moved by 1% of the time
where the time goes in v4:
time: 159 us; the launch traced here: 156 us
  Pallas kernels  146 us (92%)
  other arithmetic  4.51 us (3%)
  local copies, waits for them, and re-layouts  4.39 us (3%)
    pallas_call x1, Pallas kernels, layer(): pl.pallas_call(kernel, out_shape=[S((1, T, D), BF), S((1, T, D), F32), S(...  146 us

profile of v4, /device:TPU:0, one launch (start us, length us, event | category | flops | bytes accessed | tf_op | source)
XLA Modules:
  0.0 155.7 jit_solution(7588721201631329832)
XLA Ops:
  0.6 0.7 convert_bitcast_fusion
  1.3 0.1 fusion
  1.4 0.6 maximum_maximum_fusion.refs_2_
  2.0 1.8 %pad_bitcast_fusion.refs_5_ = f32[808,128]{1,0:T(8,128)} fusion(f32[103024]{0:T(1024)} %param.13), kind=kLoop, calls=%fused_computation.4 | loop fusion | bytes 825792 | tf_op jit(solution)/shard_map/reshape | solution.py:918
  3.8 146.1 %layer.1 = (bf16[1,1024,512]{2,1,0:T(8,128)(2,1)}, f32[1,1024,512]{2,1,0:T(8,128)}, f32[808,128]{1,0:T(8,128)}) custom-call(s32[1,4]{1,0:T(1,128)} %refs_0_.1, s32[1,1024]{1,0:T(1,128)} %refs_1_.1, bf16[8,256]{1,0:T(8,128)(2,1)} %maximum_maximum_fusion.refs_2_, bf16[1024,512]{1,0:T(8,128)(2,1)} %bitcast.7, bf16[1024,512]{1,0:T(8,128)(2,1)} %bitcast.8, ...), custom_call_target="tpu_custom_call" | custom-call | tf_op jit(solution)/shard_map/layer/pallas_call | solution.py:878
  149.9 0.0 copy-start.3
  149.9 0.0 copy-start.2
  149.9 2.3 %fusion.2 = (bf16[103024]{0:T(1024)(128)(2,1)}, f32[103024]{0:T(1024)S(1)}, f32[103024]{0:T(1024)}) fusion(f32[103024]{0:T(1024)} %param.13, f32[103424]{0:T(1024)} %bitcast.9, f32[103024]{0:T(1024)} %param.14), kind=kLoop, calls=%fused_computation.12 | loop fusion | flops 824192 | bytes 2266528 | tf_op jit(solution)/shard_map/convert_element_type | solution.py:934
  152.2 0.0 copy-start.1
  152.2 0.0 copy-start
  152.2 0.0 copy-done.3
  152.2 0.8 multiply_add_fusion
  153.1 0.0 copy-done.2
  153.1 1.0 copy.16
  154.0 0.3 copy-done
  154.3 1.3 copy.17
  155.7 0.0 copy-done.1
  (1 shorter events, 0.0 us)
Async XLA Ops:
  149.9 2.3 %copy-start.3 = (f32[103024]{0:T(1024)S(1)}, f32[103024]{0:T(1024)}, u32[]{:S(2)}) copy-start(f32[103024]{0:T(1024)} %param.15) | copy-start | bytes 1236292
  149.9 3.1 %copy-start.2 = (bf16[1,1024,512]{2,1,0:T(8,128)(2,1)S(1)}, bf16[1,1024,512]{2,1,0:T(8,128)(2,1)}, u32[]{:S(2)}) copy-start(bf16[1,1024,512]{2,1,0:T(8,128)(2,1)} %get-tuple-element.23) | copy-start | bytes 3145732
  152.2 3.4 %copy-start.1 = (f32[103024]{0:T(1024)}, f32[103024]{0:T(1024)S(1)}, u32[]{:S(2)}) copy-start(f32[103024]{0:T(1024)S(1)} %get-tuple-element.25) | copy-start | bytes 1236292
  152.2 2.1 %copy-start = (f32[1,1024,512]{2,1,0:T(8,128)S(1)}, f32[1,1024,512]{2,1,0:T(8,128)}, u32[]{:S(2)}) copy-start(f32[1,1024,512]{2,1,0:T(8,128)} %get-tuple-element.24) | copy-start | bytes 6291460
